TPU v7x, 128 devices: a whole 4x4x4 slice. The times are simulated.
128 devices in a mesh: seq: 32 (over z_hi, y, x), ch: 4 (over z_lo, core).
Axes of the slice: x: 4, y: 4, z: 4 (z_hi: 2, z_lo: 2; z = z_hi * 2 + z_lo), core: 2. Of those that a mesh axis runs over, the one named last changes fastest.
Arguments:
- tokens: bfloat16 [262144, 512], P('seq', 'ch'), may hold values from -6 to 6
- gate: bfloat16 [262144, 512], P('seq', 'ch'), may hold values from -6 to 6
- cotangent: bfloat16 [262144, 512], P('seq', 'ch'), may hold values from -6 to 6
- w_first: bfloat16 [1024, 1024], replicated, may hold values from -0.1875 to 0.1875
- w_second: bfloat16 [256, 256], replicated, may hold values from -0.375 to 0.375
Outputs:
- mixed: bfloat16 [262144, 512], P('seq', 'ch')
- grad_tokens: bfloat16 [262144, 512], P('seq', 'ch')
- grad_gate: bfloat16 [262144, 512], P('seq', 'ch')
- grad_first: float32 [1024, 1024], replicated
- grad_second: float32 [256, 256], replicated
All inputs are finite; a program needn't handle non-finite values.
Results may differ from a plain program's by a relative error of at most 0.0058.
Values may be sent and summed in bfloat16 or wider, within the bound.
No kernel may reach another device: no remote copies, remote signals or barrier semaphores. Data moves between devices by JAX's collectives and lax.ppermute only.
A program may use at most 128 MiB of HBM per device.

v0:
```python
import jax
import jax.numpy as jnp
from jax import lax
from jax.sharding import PartitionSpec as P


def local(tokens, gate, cotangent, w_first, w_second):
    seq_count = lax.axis_size("seq")
    chan_count = lax.axis_size("ch")
    width = tokens.shape[1]
    block = w_first.shape[0]
    local_blocks = tokens.shape[0] // block
    all_blocks = local_blocks * seq_count
    x_blocks = tokens.reshape(local_blocks, block, width)
    gate_f = gate.reshape(local_blocks, block, width).astype(jnp.float32)
    cot_blocks = cotangent.reshape(local_blocks, block, width)
    first = jnp.einsum("jk,ikc->ijc", w_first, x_blocks, preferred_element_type=jnp.float32)
    sig = jax.nn.sigmoid(gate_f)
    act = gate_f * sig
    slope = sig * (1.0 + gate_f * (1.0 - sig))
    hidden = (first * act).astype(jnp.bfloat16)
    hidden_t = lax.all_to_all(hidden, "seq", split_axis=1, concat_axis=0, tiled=True)
    mixed_t = jnp.einsum(
        "il,ljc->ijc", w_second, hidden_t, preferred_element_type=jnp.float32
    ).astype(jnp.bfloat16)
    mixed = lax.all_to_all(mixed_t, "seq", split_axis=0, concat_axis=1, tiled=True)
    cot_t = lax.all_to_all(cot_blocks, "seq", split_axis=1, concat_axis=0, tiled=True)
    grad_hidden_t = jnp.einsum(
        "il,ijc->ljc", w_second, cot_t, preferred_element_type=jnp.float32
    ).astype(jnp.bfloat16)
    grad_hidden = lax.all_to_all(grad_hidden_t, "seq", split_axis=0, concat_axis=1, tiled=True)
    second_term = jnp.einsum("ijc,ljc->il", cot_t, hidden_t, preferred_element_type=jnp.float32)
    gh_float = grad_hidden.astype(jnp.float32)
    grad_first_act = (gh_float * act).astype(jnp.bfloat16)
    grad_gate = (gh_float * first * slope).astype(jnp.bfloat16)
    grad_tokens = jnp.einsum(
        "jk,ijc->ikc", w_first, grad_first_act, preferred_element_type=jnp.float32
    ).astype(jnp.bfloat16)
    first_term = jnp.einsum(
        "ijc,ikc->jk", grad_first_act, x_blocks, preferred_element_type=jnp.float32
    )
    first_sum, second_sum = lax.psum((first_term, second_term), ("seq", "ch"))
    total_width = width * chan_count
    grad_first = first_sum / jnp.sqrt(jnp.float32(all_blocks * total_width))
    grad_second = second_sum / jnp.sqrt(jnp.float32(block * total_width))
    rows = local_blocks * block
    return (
        mixed.reshape(rows, width),
        grad_tokens.reshape(rows, width),
        grad_gate.reshape(rows, width),
        grad_first,
        grad_second,
    )


def solution(mesh):
    return jax.shard_map(
        local,
        mesh=mesh,
        in_specs=(P("seq", "ch"), P("seq", "ch"), P("seq", "ch"), P(), P()),
        out_specs=(P("seq", "ch"), P("seq", "ch"), P("seq", "ch"), P(), P()),
        check_vma=False,
    )
```

profile of v0, /device:TPU:1, one launch (start us, length us, event | category | flops | bytes accessed | tf_op | source)
XLA Modules:
  0.0 332.1 jit_solution(3215558701580187851)
XLA Ops:
  7.2 3.1 copy.85
  10.3 39.3 %all_to_all.60 = bf16[8,1024,128]{2,0,1:T(8,128)(2,1)S(1)} all-to-all(bf16[8,1024,128]{2,0,1:T(8,128)(2,1)S(1)} %copy.85), channel_id=1, replica_groups=mesh['seq'=32,'ch'=4] {'seq'}, dimensions={1} | all-to-all | bytes 4194304 | tf_op jit(solution)/shard_map/all_to_all | solution.py:27
  49.6 1.4 copy-done.2
  51.0 0.7 fusion.14
  51.7 2.7 copy.89
  54.4 4.8 %all-to-all-start.3 = ((bf16[256,32,128]{2,1,0:T(8,128)(2,1)}), bf16[256,32,128]{2,1,0:T(8,128)(2,1)}, u32[]{:S(2)}, u32[]{:S(2)}) async-start(bf16[256,32,128]{2,1,0:T(8,128)(2,1)} %copy.89), calls=%async_computation.3 | async-start | bytes 4194304 | tf_op jit(solution)/shard_map/all_to_all | solution.py:31
  59.2 4.1 %copy.78 = f32[8,1024,128]{1,2,0:T(8,128)} copy(bf16[8,1024,128]{2,1,0:T(8,128)(2,1)} %bitcast.77) | data formatting | bytes 6291456 | tf_op jit(solution)/shard_map/convert_element_type | solution.py:15
  63.3 23.5 %all-to-all-done.3 = bf16[256,32,128]{2,1,0:T(8,128)(2,1)} async-done(((bf16[256,32,128]{2,1,0:T(8,128)(2,1)}), bf16[256,32,128]{2,1,0:T(8,128)(2,1)}, u32[]{:S(2)}, u32[]{:S(2)}) %all-to-all-start.3) | async-done | bytes 2097184 | tf_op jit(solution)/shard_map/all_to_all | solution.py:31
  86.8 2.1 convert_bitcast_fusion
  88.9 2.6 copy.90
  91.6 5.4 %copy.91 = f32[8,1024,128]{1,2,0:T(8,128)} copy(f32[8,1024,128]{2,1,0:T(8,128)} %bitcast.71) | data formatting | bytes 8388608 | tf_op jit(solution)/shard_map/convert_element_type | solution.py:33
  97.0 8.7 %fusion.2 = (bf16[8,1024,128]{1,2,0:T(8,128)(2,1)}, bf16[8,1024,128]{1,2,0:T(8,128)(2,1)}, bf16[8,1024,128]{1,2,0:T(8,128)(2,1)}) fusion(f32[8,1024,128]{1,2,0:T(8,128)} %copy.91, f32[8,1024,128]{1,2,0:T(8,128)} %copy.78, bf16[8,1024,128]{2,1,0:T(8,128)(2,1)S(1)} %bitcast.69, bf16[1024,1024]{1,0:T(8,128)(2,1)} %param.8), kind=kOutput, calls=%fused_computation.5 | convolution fusion | flops 2163212288 | bytes 18874368 | tf_op jit(solution)/shard_map/jk,ikc->ijc/dot_general | solution.py:17
  105.6 4.2 %copy.79 = bf16[8,1024,128]{2,0,1:T(8,128)(2,1)} copy(bf16[8,1024,128]{1,2,0:T(8,128)(2,1)} %get-tuple-element.33) | data formatting | bytes 4194304 | tf_op jit(solution)/shard_map/convert_element_type | solution.py:21
  109.8 4.8 %all-to-all-start = ((bf16[8,1024,128]{2,0,1:T(8,128)(2,1)}), bf16[8,1024,128]{2,0,1:T(8,128)(2,1)}, u32[]{:S(2)}, u32[]{:S(2)}) async-start(bf16[8,1024,128]{2,0,1:T(8,128)(2,1)} %copy.79), calls=%async_computation | async-start | bytes 4194304 | tf_op jit(solution)/shard_map/all_to_all | solution.py:22
  114.6 0.2 all-reduce.3.cloned.1.call-start
  114.8 6.0 %convolution_bitcast_fusion = f32[1024,1024]{1,0:T(8,128)} fusion(bf16[8,1024,128]{1,2,0:T(8,128)(2,1)} %get-tuple-element.34, bf16[8,1024,128]{2,1,0:T(8,128)(2,1)S(1)} %bitcast.70), kind=kOutput, calls=%fused_computation.9 | convolution fusion | flops 2147483648 | bytes 8388608 | tf_op jit(solution)/shard_map/ijc,ikc->jk/dot_general | solution.py:39
  120.8 19.4 %all-to-all-done = bf16[8,1024,128]{2,0,1:T(8,128)(2,1)} async-done(((bf16[8,1024,128]{2,0,1:T(8,128)(2,1)}), bf16[8,1024,128]{2,0,1:T(8,128)(2,1)}, u32[]{:S(2)}, u32[]{:S(2)}) %all-to-all-start) | async-done | bytes 2097184 | tf_op jit(solution)/shard_map/all_to_all | solution.py:22
  140.2 2.2 copy.81
  142.4 1.3 copy-done.4
  143.7 1.7 fusion.21
  145.4 1.6 copy-done.5
  147.0 3.0 convert_bitcast_fusion.2
  150.0 4.6 %copy.83 = bf16[256,32,128]{2,1,0:T(8,128)(2,1)} copy(bf16[256,32,128]{0,2,1:T(8,128)(2,1)} %convert_bitcast_fusion.2) | data formatting | bytes 4194304 | tf_op jit(solution)/shard_map/convert_element_type | solution.py:25
  154.6 5.4 %all-to-all-start.1 = ((bf16[256,32,128]{2,1,0:T(8,128)(2,1)}), bf16[256,32,128]{2,1,0:T(8,128)(2,1)S(1)}, u32[]{:S(2)}, u32[]{:S(2)}) async-start(bf16[256,32,128]{2,1,0:T(8,128)(2,1)} %copy.83), calls=%async_computation.1 | async-start | bytes 4194304 | tf_op jit(solution)/shard_map/all_to_all | solution.py:26
  160.0 3.9 %copy.95 = bf16[8,1024,128]{2,1,0:T(8,128)(2,1)} copy(bf16[8,1024,128]{1,2,0:T(8,128)(2,1)} %get-tuple-element.32) | data formatting | bytes 4194304 | tf_op jit(solution)/shard_map/convert_element_type | solution.py:35
  163.9 6.0 %convert_bitcast_fusion.1 = bf16[8,1024,128]{1,2,0:T(8,128)(2,1)} fusion(bf16[8,1024,128]{1,2,0:T(8,128)(2,1)} %get-tuple-element.34, bf16[1024,1024]{1,0:T(8,128)(2,1)} %param.8), kind=kOutput, calls=%fused_computation.19 | convolution fusion | flops 2148532224 | bytes 6291456 | tf_op jit(solution)/shard_map/jk,ijc->ikc/dot_general | solution.py:36
  169.9 3.9 %copy.92 = bf16[8,1024,128]{2,1,0:T(8,128)(2,1)} copy(bf16[8,1024,128]{1,2,0:T(8,128)(2,1)} %convert_bitcast_fusion.1) | data formatting | bytes 4194304 | tf_op jit(solution)/shard_map/convert_element_type | solution.py:38
  173.8 15.1 %all-to-all-done.1 = bf16[256,32,128]{2,1,0:T(8,128)(2,1)S(1)} async-done(((bf16[256,32,128]{2,1,0:T(8,128)(2,1)}), bf16[256,32,128]{2,1,0:T(8,128)(2,1)S(1)}, u32[]{:S(2)}, u32[]{:S(2)}) %all-to-all-start.1) | async-done | bytes 2097184 | tf_op jit(solution)/shard_map/all_to_all | solution.py:26
  188.9 1.8 copy.84
  190.6 128.4 %all-reduce.3.cloned.1.call-done = (f32[1024,1024]{1,0:T(8,128)}, f32[256,256]{0,1:T(8,128)}) async-done(((f32[1024,1024]{1,0:T(8,128)}, f32[256,256]{0,1:T(8,128)}), (f32[1024,1024]{1,0:T(8,128)}, f32[256,256]{0,1:T(8,128)})) %all-reduce.3.cloned.1.call-update) | async-done | bytes 4456464 | tf_op jit(solution)/shard_map/psum | solution.py:42
  319.1 5.3 %broadcast_multiply_fusion = f32[1024,1024]{1,0:T(8,128)} fusion(f32[1024,1024]{1,0:T(8,128)} %get-tuple-element.30), kind=kLoop, calls=%fused_computation.18 | loop fusion | flops 1048576 | bytes 8388608 | tf_op jit(solution)/shard_map/div | solution.py:44
  324.4 0.8 copy.98
  (15 shorter events, 0.1 us)
Async XLA Ops:
  7.2 89.8 %copy-start = (bf16[8192,128]{1,0:T(8,128)(2,1)S(1)}, bf16[8192,128]{1,0:T(8,128)(2,1)}, u32[]{:S(2)}) copy-start(bf16[8192,128]{1,0:T(8,128)(2,1)} %param.5) | copy-start | bytes 6291460
  10.3 40.7 %copy-start.6 = (bf16[256,256]{1,0:T(8,128)(2,1)S(1)}, bf16[256,256]{1,0:T(8,128)(2,1)}, u32[]{:S(2)}) copy-start(bf16[256,256]{1,0:T(8,128)(2,1)} %param.9) | copy-start | bytes 393220
  49.6 1.4 copy-start.2
  54.4 32.4 %all-to-all-start.3 = ((bf16[256,32,128]{2,1,0:T(8,128)(2,1)}), bf16[256,32,128]{2,1,0:T(8,128)(2,1)}, u32[]{:S(2)}, u32[]{:S(2)}) async-start(bf16[256,32,128]{2,1,0:T(8,128)(2,1)} %copy.89), calls=%async_computation.3 | async-start | bytes 4194304 | tf_op jit(solution)/shard_map/all_to_all | solution.py:31
  109.8 30.4 %all-to-all-start = ((bf16[8,1024,128]{2,0,1:T(8,128)(2,1)}), bf16[8,1024,128]{2,0,1:T(8,128)(2,1)}, u32[]{:S(2)}, u32[]{:S(2)}) async-start(bf16[8,1024,128]{2,0,1:T(8,128)(2,1)} %copy.79), calls=%async_computation | async-start | bytes 4194304 | tf_op jit(solution)/shard_map/all_to_all | solution.py:22
  114.6 204.5 %all-reduce.3.cloned.1.call-start = ((), (), s32[]{:S(2)}) async-start(), calls=%async_computation.4 | async-start | bytes 8912896 | tf_op jit(solution)/shard_map/psum | solution.py:42
  140.2 3.5 %copy-start.3 = (bf16[8,1024,128]{2,0,1:T(8,128)(2,1)S(1)}, bf16[8,1024,128]{2,0,1:T(8,128)(2,1)}, u32[]{:S(2)}) copy-start(bf16[8,1024,128]{2,0,1:T(8,128)(2,1)} %copy-done.2) | copy-start | bytes 6291460
  142.4 1.3 copy-start.4
  145.4 1.6 copy-start.5
  154.6 34.3 %all-to-all-start.1 = ((bf16[256,32,128]{2,1,0:T(8,128)(2,1)}), bf16[256,32,128]{2,1,0:T(8,128)(2,1)S(1)}, u32[]{:S(2)}, u32[]{:S(2)}) async-start(bf16[256,32,128]{2,1,0:T(8,128)(2,1)} %copy.83), calls=%async_computation.1 | async-start | bytes 4194304 | tf_op jit(solution)/shard_map/all_to_all | solution.py:26
  319.1 5.3 %copy-start.7 = (f32[256,256]{0,1:T(8,128)S(1)}, f32[256,256]{0,1:T(8,128)}, u32[]{:S(2)}) copy-start(f32[256,256]{0,1:T(8,128)} %get-tuple-element.31) | copy-start | bytes 786436
  319.1 6.1 %copy-start.1 = (bf16[8192,128]{1,0:T(8,128)(2,1)S(1)}, bf16[8192,128]{1,0:T(8,128)(2,1)}, u32[]{:S(2)}) copy-start(bf16[8192,128]{1,0:T(8,128)(2,1)} %param.5) | copy-start | bytes 6291460
Sparse Core Ops, SparseCore 0:
  145.5 173.4 all-reduce.2
where the time goes:
time: 333 us; the launch traced here: 332 us
  waiting for transfers between devices  186 us (56%)
  local copies, waits for them, and re-layouts  43.6 us (13%)
  blocking collectives  39.3 us (12%)
  matrix products  26 us (8%)
  starting transfers between devices  15.2 us (5%)
  between operations  14.1 us (4%)
  other arithmetic  7.44 us (2%)
    psum x1, waiting for transfers between devices, local(): first_sum, second_sum = lax.psum((first_term, second_term), ('seq', 'ch'))  128 us
    all_to_all x1, blocking collectives, local(): lax.all_to_all(cot_blocks, 'seq', split_axis=1, concat_axis=0, tiled=True)  39.3 us
    all_to_all x1, waiting for transfers between devices, local(): lax.all_to_all(grad_hidden_t, 'seq', split_axis=0, concat_axis=1, tiled=T...  23.5 us
    all_to_all x1, waiting for transfers between devices, local(): lax.all_to_all(hidden, 'seq', split_axis=1, concat_axis=0, tiled=True)  19.4 us
    all_to_all x1, waiting for transfers between devices, local(): lax.all_to_all(mixed_t, 'seq', split_axis=0, concat_axis=1, tiled=True)  15.1 us
    dot_general x1, matrix products, local(): jnp.einsum('jk,ikc->ijc', w_first, x_blocks, preferred_element_type=jnp.f...  8.67 us
    convert_element_type x2, local copies, waits for them, and re-layouts, local(): gh_float = grad_hidden.astype(jnp.float32)  8.05 us
  transfers between devices with their start and end apart: 4, of which 4 were waited for; matrix products, arithmetic and copies ran while one was open for 10% of the time, Pallas kernels for 0%

commit v1 on v0

v1 whole, which is shorter than its diff:
```python
import jax
import jax.numpy as jnp
from jax import lax
from jax.experimental import pallas as pl
from jax.experimental.pallas import tpu as pltpu
from jax.sharding import PartitionSpec as P

BF = jnp.bfloat16
F32 = jnp.float32
LANES = 128


def gates(g):
    sig = jax.nn.sigmoid(g)
    return g * sig, sig * (1.0 + g * (1.0 - sig))


def front(x, g, w_first, tj):
    lb, block, width = x.shape

    def body(x_ref, g_ref, w_ref, hid_ref, first_ref, wide, turn):
        @pl.when(pl.program_id(0) == 0)
        def _():
            for i in range(lb):
                wide[:, i * width : (i + 1) * width] = x_ref[i]

        res = jnp.dot(w_ref[...], wide[...], preferred_element_type=F32)
        for i in range(lb):
            part = res[:, i * width : (i + 1) * width]
            first_ref[i] = part
            act, _ = gates(g_ref[i].astype(F32))
            turn[pl.ds(i, tj, stride=lb), :] = part * act
        hid_ref[...] = turn[...].reshape(tj, lb, width).astype(BF)

    return pl.pallas_call(
        body,
        grid=(block // tj,),
        in_specs=[
            pl.BlockSpec((lb, block, width), lambda j: (0, 0, 0)),
            pl.BlockSpec((lb, tj, width), lambda j: (0, j, 0)),
            pl.BlockSpec((tj, block), lambda j: (j, 0)),
        ],
        out_specs=[
            pl.BlockSpec((tj, lb, width), lambda j: (j, 0, 0)),
            pl.BlockSpec((lb, tj, width), lambda j: (0, j, 0)),
        ],
        out_shape=[
            jax.ShapeDtypeStruct((block, lb, width), BF),
            jax.ShapeDtypeStruct((lb, block, width), F32),
        ],
        scratch_shapes=[
            pltpu.VMEM((block, lb * width), BF),
            pltpu.VMEM((tj * lb, width), F32),
        ],
        name="front",
    )(x, g, w_first)


def columns(ref, j, rows):
    return ref[:, j].astype(F32).reshape(rows, LANES).astype(BF)


def middle_back(cot_t, w_second_t, tj):
    seq, jp, lb, width = cot_t.shape
    nb = seq * lb

    def body(cot_ref, w_ref, out_ref):
        w = w_ref[...]
        for j in range(0, tj, 2):
            pair = jnp.concatenate([columns(cot_ref, j, nb), columns(cot_ref, j + 1, nb)], axis=1)
            res = jnp.dot(w, pair, preferred_element_type=F32)
            for k in range(2):
                part = res[:, k * width : (k + 1) * width]
                out_ref[:, j + k] = part.reshape(seq, lb, width).astype(BF)

    block = pl.BlockSpec((seq, tj, lb, width), lambda j: (0, j, 0, 0))
    return pl.pallas_call(
        body,
        grid=(jp // tj,),
        in_specs=[block, pl.BlockSpec((nb, nb), lambda j: (0, 0))],
        out_specs=block,
        out_shape=jax.ShapeDtypeStruct(cot_t.shape, BF),
        name="middle_back",
    )(cot_t, w_second_t)


def middle_forward(hid_t, cot_t, w_second, tj):
    seq, jp, lb, width = cot_t.shape
    nb = seq * lb
    steps = jp // tj

    def body(hid_ref, cot_ref, w_ref, out_ref, second_ref, acc):
        step = pl.program_id(0)
        w = w_ref[...]
        total = jnp.zeros((nb, nb), F32)
        for j in range(0, tj, 2):
            pair = jnp.concatenate([columns(hid_ref, j, nb), columns(hid_ref, j + 1, nb)], axis=1)
            res = jnp.dot(w, pair, preferred_element_type=F32)
            for k in range(2):
                part = res[:, k * width : (k + 1) * width]
                out_ref[:, j + k] = part.reshape(seq, lb, width).astype(BF)
            cots = jnp.concatenate([columns(cot_ref, j, nb), columns(cot_ref, j + 1, nb)], axis=1)
            total += lax.dot_general(
                cots, pair, (((1,), (1,)), ((), ())), preferred_element_type=F32
            )

        @pl.when(step == 0)
        def _():
            acc[...] = total

        @pl.when(step > 0)
        def _():
            acc[...] += total

        @pl.when(step == steps - 1)
        def _():
            for k in range(nb // LANES):
                part = acc[:, k * LANES : (k + 1) * LANES]
                second_ref[:, k] = part.reshape(nb // 8, 8, LANES).astype(BF)

    block = pl.BlockSpec((seq, tj, lb, width), lambda j: (0, j, 0, 0))
    tiles = (nb // 8, nb // LANES, 8, LANES)
    return pl.pallas_call(
        body,
        grid=(steps,),
        in_specs=[block, block, pl.BlockSpec((nb, nb), lambda j: (0, 0))],
        out_specs=[block, pl.BlockSpec(tiles, lambda j: (0, 0, 0, 0))],
        out_shape=[
            jax.ShapeDtypeStruct(cot_t.shape, BF),
            jax.ShapeDtypeStruct(tiles, BF),
        ],
        scratch_shapes=[pltpu.VMEM((nb, nb), F32)],
        name="middle_forward",
    )(hid_t, cot_t, w_second)


def back(core, gh, first, x, g, w_first, tj):
    lb, block, width = x.shape
    steps = block // tj
    half = steps // 2
    tiles = block // LANES

    def body(core_ref, gh_ref, first_ref, x_ref, g_ref, w_ref, gate_ref, tok_ref, term_ref,
             wide, gfa, turn):
        step = pl.program_id(0)
        jb = (step + (1 - core_ref[0]) * half) % steps

        @pl.when(step == 0)
        def _():
            for i in range(lb):
                wide[:, i * width : (i + 1) * width] = x_ref[i]

        turn[...] = gh_ref[...].astype(F32).reshape(tj * lb, width)
        at = pl.multiple_of(jb * tj, tj)
        for i in range(lb):
            gh_i = turn[pl.ds(i, tj, stride=lb), :]
            act, slope = gates(g_ref[i].astype(F32))
            gfa[pl.ds(at, tj), i * width : (i + 1) * width] = (gh_i * act).astype(BF)
            gate_ref[i] = (gh_i * first_ref[i] * slope).astype(BF)
        term = lax.dot_general(
            gfa[pl.ds(at, tj), :], wide[...], (((1,), (1,)), ((), ())), preferred_element_type=F32
        )
        for k in range(tiles):
            part = term[:, k * LANES : (k + 1) * LANES]
            term_ref[:, k] = part.reshape(tj // 8, 8, LANES).astype(BF)

        @pl.when(step == steps - 1)
        def _():
            for i in range(0, lb, 2):
                res = lax.dot_general(
                    w_ref[...], gfa[:, i * width : (i + 2) * width],
                    (((0,), (0,)), ((), ())), preferred_element_type=F32,
                )
                tok_ref[i] = res[:, :width].astype(BF)
                tok_ref[i + 1] = res[:, width:].astype(BF)

    def at_block(j, core_ref):
        return (j + (1 - core_ref[0]) * half) % steps

    grid_spec = pltpu.PrefetchScalarGridSpec(
        num_scalar_prefetch=1,
        grid=(steps,),
        in_specs=[
            pl.BlockSpec((tj, lb, width), lambda j, c: (at_block(j, c), 0, 0)),
            pl.BlockSpec((lb, tj, width), lambda j, c: (0, at_block(j, c), 0)),
            pl.BlockSpec((lb, block, width), lambda j, c: (0, 0, 0)),
            pl.BlockSpec((lb, tj, width), lambda j, c: (0, at_block(j, c), 0)),
            pl.BlockSpec((block, block), lambda j, c: (0, 0)),
        ],
        out_specs=[
            pl.BlockSpec((lb, tj, width), lambda j, c: (0, at_block(j, c), 0)),
            pl.BlockSpec((lb, block, width), lambda j, c: (0, 0, 0)),
            pl.BlockSpec((tj // 8, tiles, 8, LANES), lambda j, c: (j, 0, 0, 0)),
        ],
        scratch_shapes=[
            pltpu.VMEM((block, lb * width), BF),
            pltpu.VMEM((block, lb * width), BF),
            pltpu.VMEM((tj * lb, width), F32),
        ],
    )
    return pl.pallas_call(
        body,
        grid_spec=grid_spec,
        out_shape=[
            jax.ShapeDtypeStruct((lb, block, width), BF),
            jax.ShapeDtypeStruct((lb, block, width), BF),
            jax.ShapeDtypeStruct((block // 8, tiles, 8, LANES), BF),
        ],
        name="back",
    )(core, gh, first, x, g, w_first)


def pair_sum(term, taken, second, chips):
    tiles = term.shape[1]

    def body(own_ref, taken_ref, second_ref, out_ref):
        out_ref[:, :tiles] = (own_ref[...].astype(F32) + taken_ref[...].astype(F32)).astype(BF)
        out_ref[:, tiles] = second_ref[...]

    step = chips // 4
    return pl.pallas_call(
        body,
        grid=(4,),
        in_specs=[
            pl.BlockSpec((step, tiles, 8, LANES), lambda p: (p + 4, 0, 0, 0)),
            pl.BlockSpec((step, tiles, 8, LANES), lambda p: (p, 0, 0, 0)),
            pl.BlockSpec((step, 8, LANES), lambda p: (p, 0, 0)),
        ],
        out_specs=pl.BlockSpec((step, tiles + 1, 8, LANES), lambda p: (p, 0, 0, 0)),
        out_shape=jax.ShapeDtypeStruct((chips, tiles + 1, 8, LANES), BF),
        name="pair_sum",
    )(term, taken, second)


def chip_sum(parts):
    def body(in_ref, out_ref):
        total = jnp.sum(in_ref[...].astype(F32), axis=0).astype(BF)
        out_ref[...] = jnp.broadcast_to(total[None], out_ref.shape)

    return pl.pallas_call(
        body, out_shape=jax.ShapeDtypeStruct(parts.shape, BF), name="chip_sum"
    )(parts)


def unpack(core, mine, other, block, nb, scale_first, scale_second):
    chips, tiles = mine.shape[0], mine.shape[1] - 1
    step = chips // 4
    lane_tiles = nb // LANES

    def body(core_ref, mine_ref, other_ref, first_ref, second_ref):
        use_mine = core_ref[0] == pl.program_id(0)

        @pl.when(use_mine)
        def _():
            for k in range(tiles):
                part = mine_ref[:, k].astype(F32) * scale_first
                first_ref[:, k * LANES : (k + 1) * LANES] = part.reshape(step * 8, LANES)

        @pl.when(jnp.logical_not(use_mine))
        def _():
            for k in range(tiles):
                part = other_ref[:, k].astype(F32) * scale_first
                first_ref[:, k * LANES : (k + 1) * LANES] = part.reshape(step * 8, LANES)

        both = mine_ref[:, tiles].astype(F32) + other_ref[:, tiles].astype(F32)
        both = (both * scale_second).reshape(step // lane_tiles, lane_tiles, 8, LANES)
        for k in range(lane_tiles):
            second_ref[:, k * LANES : (k + 1) * LANES] = both[:, k].reshape(-1, LANES)

    spec = pl.BlockSpec((step, tiles + 1, 8, LANES), lambda h, p, c: (p, 0, 0, 0))
    grid_spec = pltpu.PrefetchScalarGridSpec(
        num_scalar_prefetch=1,
        grid=(2, 4),
        in_specs=[spec, spec],
        out_specs=[
            pl.BlockSpec((step * 8, block), lambda h, p, c: (h * 4 + p, 0)),
            pl.BlockSpec((step // lane_tiles * 8, nb), lambda h, p, c: (p, 0)),
        ],
    )
    return pl.pallas_call(
        body,
        grid_spec=grid_spec,
        out_shape=[
            jax.ShapeDtypeStruct((block, block), F32),
            jax.ShapeDtypeStruct((nb, nb), F32),
        ],
        name="unpack",
    )(core, mine, other)


def local(tokens, gate, cotangent, w_first, w_second):
    seq_count = lax.axis_size("seq")
    chan_count = lax.axis_size("ch")
    width = tokens.shape[1]
    block = w_first.shape[0]
    lb = tokens.shape[0] // block
    nb = lb * seq_count
    jp = block // seq_count
    rows = lb * block
    chips = seq_count * chan_count // 2
    same_core = [[2 * k + core for k in range(chips)] for core in range(2)]
    pairs = [(i, i ^ 1) for i in range(chan_count)]
    core = (lax.axis_index("ch") % 2).astype(jnp.int32).reshape(1)

    def exchange(x):
        return lax.all_to_all(x, "seq", split_axis=0, concat_axis=0, tiled=True)

    def chip_exchange(x):
        return lax.all_to_all(
            x, ("seq", "ch"), 0, 0, tiled=True, axis_index_groups=same_core
        )

    x = tokens.reshape(lb, block, width)
    g = gate.reshape(lb, block, width)
    cot = cotangent.reshape(lb, seq_count, jp, width).transpose(1, 2, 0, 3)
    cot_t = exchange(cot)
    hidden, first = front(x, g, w_first, 128)
    hid_t = exchange(hidden.reshape(seq_count, jp, lb, width))
    gh_t = middle_back(cot_t, w_second.T, 8)
    gh_t, hid_t = lax.optimization_barrier((gh_t, hid_t))
    gh_r = exchange(gh_t).reshape(block, lb, width)
    mixed_t, second_term = middle_forward(hid_t, cot_t, w_second, 8)
    mixed_t, gh_r = lax.optimization_barrier((mixed_t, gh_r))
    mixed_r = exchange(mixed_t).reshape(block, lb, width)
    grad_gate, grad_tokens, term = back(core, gh_r, first, x, g, w_first, 128)
    taken = lax.ppermute(term[:chips], "ch", pairs)
    part = pair_sum(term, taken, second_term.reshape(chips, 8, LANES), chips)
    part, mixed_r = lax.optimization_barrier((part, mixed_r))
    part = chip_exchange(part)
    mixed = mixed_r.transpose(1, 0, 2).reshape(rows, width)
    mine = chip_exchange(chip_sum(part))
    other = lax.ppermute(mine, "ch", pairs)
    total_width = width * chan_count
    grad_first, grad_second = unpack(
        core, mine, other, block, nb,
        (nb * total_width) ** -0.5, (block * total_width) ** -0.5,
    )
    return mixed, grad_tokens.reshape(rows, width), grad_gate.reshape(rows, width), grad_first, grad_second


def solution(mesh):
    return jax.shard_map(
        local,
        mesh=mesh,
        in_specs=(P("seq", "ch"), P("seq", "ch"), P("seq", "ch"), P(), P()),
        out_specs=(P("seq", "ch"), P("seq", "ch"), P("seq", "ch"), P(), P()),
        check_vma=False,
    )
```

time: 333 us -> 219 us (0.66)
  waiting for transfers between devices: 186 us -> 68.8 us
  Pallas kernels: 0 us -> 48.8 us
  local copies, waits for them, and re-layouts: 43.6 us -> 15.2 us
  matrix products: 26 us -> 0 us
  starting transfers between devices: 15.2 us -> 33.7 us
  between operations: 14.1 us -> 0.7 us
  blocking collectives: 39.3 us -> 49.8 us
  other arithmetic: 7.44 us -> 0 us
    psum x1 -> x0, waiting for transfers between devices: 128 us -> none  [local(): first_sum, second_sum = lax.psum((first_term, second_term), ('seq', 'ch'))]
    pallas_call x0 -> x7, Pallas kernels: none -> 48.8 us  [the longest x1 16.2 us: back(): pl.pallas_call(body, grid_spec=grid_spec, out_shape=[jax.ShapeDtypeStruct...]
    convert_element_type x8 -> x0, local copies, waits for them, and re-layouts: 31.4 us -> none  [the longest x2 8.05 us: local(): gh_float = grad_hidden.astype(jnp.float32)]
    dot_general x6 -> x0, matrix products: 26 us -> none  [the longest x1 8.67 us: local(): jnp.einsum('jk,ikc->ijc', w_first, x_blocks, preferred_element_type=jnp.f...]
    all_to_all x3 -> x4, starting transfers between devices: 15 us -> 29.1 us  [exchange(): return lax.all_to_all(x, 'seq', split_axis=0, concat_axis=0, tiled=True)]
    all_to_all x1 -> x2, blocking collectives: 39.3 us -> 49.8 us  [chip_exchange(): lax.all_to_all(x, ('seq', 'ch'), 0, 0, tiled=True, axis_index_groups=same...]
    all_to_all x3 -> x4, waiting for transfers between devices: 57.9 us -> 66.5 us  [exchange(): return lax.all_to_all(x, 'seq', split_axis=0, concat_axis=0, tiled=True)]
    div x2 -> x0, other arithmetic: 5.3 us -> none  [the longest x1 5.27 us: local(): grad_first = first_sum / jnp.sqrt(jnp.float32(all_blocks * total_width))]
  transfers between devices with their start and end apart: 4 -> 6, of which waited for: 4 -> 5; matrix products, arithmetic and copies ran while one was open for 10% -> 2% of each run, Pallas kernels for 0% -> 18%
where the time goes in v1:
time: 219 us; the launch traced here: 217 us
  waiting for transfers between devices  68.8 us (31%)
  blocking collectives  49.8 us (23%)
  Pallas kernels  48.8 us (22%)
  starting transfers between devices  33.7 us (15%)
  local copies, waits for them, and re-layouts  15.2 us (7%)
    all_to_all x4, waiting for transfers between devices, exchange(): return lax.all_to_all(x, 'seq', split_axis=0, concat_axis=0, tiled=True)  66.5 us
    all_to_all x2, blocking collectives, chip_exchange(): lax.all_to_all(x, ('seq', 'ch'), 0, 0, tiled=True, axis_index_groups=same...  49.8 us
    all_to_all x4, starting transfers between devices, exchange(): return lax.all_to_all(x, 'seq', split_axis=0, concat_axis=0, tiled=True)  29.1 us
    pallas_call x1, Pallas kernels, back(): pl.pallas_call(body, grid_spec=grid_spec, out_shape=[jax.ShapeDtypeStruct...  16.2 us
    pallas_call x1, Pallas kernels, front(): pl.pallas_call(body, grid=(block // tj,), in_specs=[pl.BlockSpec((lb, blo...  9.99 us
    pallas_call x1, Pallas kernels, unpack(): pl.pallas_call(body, grid_spec=grid_spec, out_shape=[jax.ShapeDtypeStruct...  6.88 us
    unnamed x13, local copies, waits for them, and re-layouts  5.41 us
    reshape x1, local copies, waits for them, and re-layouts, local(): cot = cotangent.reshape(lb, seq_count, jp, width).transpose(1, 2, 0, 3)  5.34 us
  transfers between devices with their start and end apart: 6, of which 5 were waited for; matrix products, arithmetic and copies ran while one was open for 2% of the time, Pallas kernels for 18%

profile of v1, /device:TPU:1, one launch (start us, length us, event | category | flops | bytes accessed | tf_op | source)
XLA Modules:
  0.0 217.1 jit_solution(8658257393197426855)
XLA Ops:
  0.6 5.3 %copy.16 = bf16[8,32,32,128]{3,0,2,1:T(8,128)(2,1)} copy(bf16[8,32,32,128]{3,2,1,0:T(8,128)(2,1)} %bitcast.22) | data formatting | bytes 4194304 | tf_op jit(solution)/shard_map/reshape | solution.py:315
  6.0 11.2 %all-to-all-start = ((bf16[32,32,8,128]{3,2,1,0:T(8,128)(2,1)}), bf16[32,32,8,128]{3,2,1,0:T(8,128)(2,1)S(1)}, u32[]{:S(2)}, u32[]{:S(2)}) async-start(bf16[32,32,8,128]{3,2,1,0:T(8,128)(2,1)} %bitcast.21), calls=%async_computation | async-start | bytes 4194304 | tf_op jit(solution)/shard_map/all_to_all | solution.py:306
  17.1 10.0 %front.1 = (bf16[1024,8,128]{2,1,0:T(8,128)(2,1)}, f32[8,1024,128]{2,1,0:T(8,128)}) custom-call(bf16[8,1024,128]{2,1,0:T(8,128)(2,1)} %bitcast.16, bf16[8,1024,128]{2,1,0:T(8,128)(2,1)} %bitcast.18, bf16[1024,1024]{1,0:T(8,128)(2,1)} %w_ref.5), custom_call_target="tpu_custom_call" | custom-call | tf_op jit(solution)/shard_map/front/pallas_call | solution.py:35
  27.1 18.4 %all-to-all-done.cot_ref = bf16[32,32,8,128]{3,2,1,0:T(8,128)(2,1)S(1)} async-done(((bf16[32,32,8,128]{3,2,1,0:T(8,128)(2,1)}), bf16[32,32,8,128]{3,2,1,0:T(8,128)(2,1)S(1)}, u32[]{:S(2)}, u32[]{:S(2)}) %all-to-all-start) | async-done | bytes 2097184 | tf_op jit(solution)/shard_map/all_to_all | solution.py:306
  45.6 0.0 copy-start.5
  45.6 1.3 copy-done
  46.9 6.0 %all-to-all-start.1 = ((bf16[32,32,8,128]{3,2,1,0:T(8,128)(2,1)}), bf16[32,32,8,128]{3,2,1,0:T(8,128)(2,1)}, u32[]{:S(2)}, u32[]{:S(2)}) async-start(bf16[32,32,8,128]{3,2,1,0:T(8,128)(2,1)} %bitcast.24), calls=%async_computation.1 | async-start | bytes 4194304 | tf_op jit(solution)/shard_map/all_to_all | solution.py:306
  52.9 0.0 copy-done.5
  52.9 0.8 copy.13
  53.6 4.4 %middle_back.1 = bf16[32,32,8,128]{3,2,1,0:T(8,128)(2,1)} custom-call(bf16[32,32,8,128]{3,2,1,0:T(8,128)(2,1)} %copy-done, bf16[256,256]{1,0:T(8,128)(2,1)} %bitcast.25), custom_call_target="tpu_custom_call" | custom-call | tf_op jit(solution)/shard_map/middle_back/pallas_call | solution.py:77
  58.0 22.7 %all-to-all-done.1.hid_ref = bf16[32,32,8,128]{3,2,1,0:T(8,128)(2,1)} async-done(((bf16[32,32,8,128]{3,2,1,0:T(8,128)(2,1)}), bf16[32,32,8,128]{3,2,1,0:T(8,128)(2,1)}, u32[]{:S(2)}, u32[]{:S(2)}) %all-to-all-start.1) | async-done | bytes 2097184 | tf_op jit(solution)/shard_map/all_to_all | solution.py:306
  80.8 6.3 %all-to-all-start.2 = ((bf16[32,32,8,128]{3,2,1,0:T(8,128)(2,1)}), bf16[32,32,8,128]{3,2,1,0:T(8,128)(2,1)S(1)}, u32[]{:S(2)}, u32[]{:S(2)}) async-start(bf16[32,32,8,128]{3,2,1,0:T(8,128)(2,1)} %middle_back.1), calls=%async_computation.2 | async-start | bytes 4194304 | tf_op jit(solution)/shard_map/all_to_all | solution.py:306
  87.0 5.1 %middle_forward.1 = (bf16[32,32,8,128]{3,2,1,0:T(8,128)(2,1)}, bf16[32,2,8,128]{3,2,1,0:T(8,128)(2,1)}) custom-call(bf16[32,32,8,128]{3,2,1,0:T(8,128)(2,1)} %all-to-all-done.1.hid_ref, bf16[32,32,8,128]{3,2,1,0:T(8,128)(2,1)} %copy-done, bf16[256,256]{1,0:T(8,128)(2,1)} %w_ref.4), custom_call_target="tpu_custom_call" | custom-call | tf_op jit(solution)/shard_map/middle_forward/pallas_call | solution.py:123
  92.1 23.4 %all-to-all-done.2 = bf16[32,32,8,128]{3,2,1,0:T(8,128)(2,1)S(1)} async-done(((bf16[32,32,8,128]{3,2,1,0:T(8,128)(2,1)}), bf16[32,32,8,128]{3,2,1,0:T(8,128)(2,1)S(1)}, u32[]{:S(2)}, u32[]{:S(2)}) %all-to-all-start.2) | async-done | bytes 2097184 | tf_op jit(solution)/shard_map/all_to_all | solution.py:306
  115.5 1.3 copy-done.1
  116.9 5.7 %all-to-all-start.3 = ((bf16[32,32,8,128]{3,2,1,0:T(8,128)(2,1)}), bf16[32,32,8,128]{3,2,1,0:T(8,128)(2,1)}, u32[]{:S(2)}, u32[]{:S(2)}) async-start(bf16[32,32,8,128]{3,2,1,0:T(8,128)(2,1)} %get-tuple-element.28), calls=%async_computation.3 | async-start | bytes 4194304 | tf_op jit(solution)/shard_map/all_to_all | solution.py:306
  122.6 16.2 %back.1 = (bf16[8,1024,128]{2,1,0:T(8,128)(2,1)}, bf16[8,1024,128]{2,1,0:T(8,128)(2,1)}, bf16[128,8,8,128]{3,2,1,0:T(8,128)(2,1)}) custom-call(s32[1]{0:T(128)} %bitcast.core_ref, bf16[1024,8,128]{2,1,0:T(8,128)(2,1)} %bitcast.20, f32[8,1024,128]{2,1,0:T(8,128)} %get-tuple-element.25.first_ref, bf16[8,1024,128]{2,1,0:T(8,128)(2,1)} %bitcast.17, ...), custom_call_target="tpu_custom_call" | custom-call | tf_op jit(solution)/shard_map/back/pallas_call | solution.py:201
  138.8 1.3 slice.3
  140.1 1.4 collective-permute-start
  141.5 2.3 %collective-permute-done.taken_ref = bf16[64,8,8,128]{3,2,1,0:T(8,128)(2,1)S(1)} collective-permute-done((bf16[64,8,8,128]{3,2,1,0:T(8,128)(2,1)S(1)}, bf16[64,8,8,128]{3,2,1,0:T(8,128)(2,1)S(1)}, u32[]{:S(2)}, u32[]{:S(2)}) %collective-permute-start) | collective-permute-done | bytes 1048608 | tf_op jit(solution)/shard_map/ppermute | solution.py:326
  143.8 1.0 copy-done.4
  144.7 3.7 %pair_sum.1 = bf16[64,9,8,128]{3,2,1,0:T(8,128)(2,1)} custom-call(bf16[128,8,8,128]{3,2,1,0:T(8,128)(2,1)} %get-tuple-element.26.own_ref, bf16[64,8,8,128]{3,2,1,0:T(8,128)(2,1)} %copy-done.4, bf16[64,8,128]{2,1,0:T(8,128)(2,1)} %bitcast.26), custom_call_target="tpu_custom_call" | custom-call | tf_op jit(solution)/shard_map/pair_sum/pallas_call | solution.py:221
  148.4 2.0 all-to-all-done.3
  150.4 26.4 %all_to_all.30.in_ref = bf16[64,9,8,128]{3,2,1,0:T(8,128)(2,1)} all-to-all(bf16[64,9,8,128]{3,2,1,0:T(8,128)(2,1)} %pair_sum.1), channel_id=1, replica_groups={{0,2,4,6,8,10,12,14,16,18,20,22,24,26,28,30,32,34,36,38,40,42,44,46,48,..., dimensions={0} | all-to-all | bytes 2359296 | tf_op jit(solution)/shard_map/all_to_all | solution.py:309
  176.8 2.5 %chip_sum.1 = bf16[64,9,8,128]{3,2,1,0:T(8,128)(2,1)} custom-call(bf16[64,9,8,128]{3,2,1,0:T(8,128)(2,1)} %all_to_all.30.in_ref), custom_call_target="tpu_custom_call" | custom-call | tf_op jit(solution)/shard_map/chip_sum/pallas_call | solution.py:240
  179.3 23.4 %all_to_all.31.mine_ref = bf16[64,9,8,128]{3,2,1,0:T(8,128)(2,1)S(1)} all-to-all(bf16[64,9,8,128]{3,2,1,0:T(8,128)(2,1)} %chip_sum.1), channel_id=1, replica_groups={{0,2,4,6,8,10,12,14,16,18,20,22,24,26,28,30,32,34,36,38,40,42,44,46,48,..., dimensions={0} | all-to-all | bytes 2359296 | tf_op jit(solution)/shard_map/all_to_all | solution.py:309
  202.7 3.2 %collective-permute-start.1 = (bf16[64,9,8,128]{3,2,1,0:T(8,128)(2,1)S(1)}, bf16[64,9,8,128]{3,2,1,0:T(8,128)(2,1)S(1)}, u32[]{:S(2)}, u32[]{:S(2)}) collective-permute-start(bf16[64,9,8,128]{3,2,1,0:T(8,128)(2,1)S(1)} %all_to_all.31.mine_ref), channel_id=1, source_target_pairs={{0,1},{1,0},{2,3},{3,2},{4,5},{5,4},{6,7},{7,6},{8,9},{9,8},{10,11... | collective-permute-start | bytes 3538952 | tf_op jit(solution)/shard_map/ppermute | solution.py:332
  205.9 3.2 %copy.14 = bf16[8,1024,128]{2,1,0:T(8,128)(2,1)} copy(bf16[8,1024,128]{2,0,1:T(8,128)(2,1)} %bitcast.10) | data formatting | bytes 4194304 | tf_op jit(solution)/shard_map/transpose | solution.py:330
  209.1 0.0 copy-done.2
  209.1 0.0 collective-permute-done.1.other_ref
  209.1 1.0 copy-done.3
  210.2 6.9 %unpack.1 = (f32[1024,1024]{1,0:T(8,128)}, f32[256,256]{1,0:T(8,128)}) custom-call(s32[1]{0:T(128)} %bitcast.core_ref, bf16[64,9,8,128]{3,2,1,0:T(8,128)(2,1)} %copy-done.2, bf16[64,9,8,128]{3,2,1,0:T(8,128)(2,1)} %copy-done.3), custom_call_target="tpu_custom_call" | custom-call | tf_op jit(solution)/shard_map/unpack/pallas_call | solution.py:280
  (5 shorter events, 0.0 us)
Async XLA Ops:
  6.0 39.6 %all-to-all-start = ((bf16[32,32,8,128]{3,2,1,0:T(8,128)(2,1)}), bf16[32,32,8,128]{3,2,1,0:T(8,128)(2,1)S(1)}, u32[]{:S(2)}, u32[]{:S(2)}) async-start(bf16[32,32,8,128]{3,2,1,0:T(8,128)(2,1)} %bitcast.21), calls=%async_computation | async-start | bytes 4194304 | tf_op jit(solution)/shard_map/all_to_all | solution.py:306
  45.6 1.3 copy-start
  45.6 7.3 %copy-start.5 = (bf16[256,256]{1,0:T(8,128)(2,1)S(1)}, bf16[256,256]{1,0:T(8,128)(2,1)}, u32[]{:S(2)}) copy-start(bf16[256,256]{1,0:T(8,128)(2,1)} %w_ref.4) | copy-start | bytes 393220
  46.9 33.9 %all-to-all-start.1 = ((bf16[32,32,8,128]{3,2,1,0:T(8,128)(2,1)}), bf16[32,32,8,128]{3,2,1,0:T(8,128)(2,1)}, u32[]{:S(2)}, u32[]{:S(2)}) async-start(bf16[32,32,8,128]{3,2,1,0:T(8,128)(2,1)} %bitcast.24), calls=%async_computation.1 | async-start | bytes 4194304 | tf_op jit(solution)/shard_map/all_to_all | solution.py:306
  80.8 34.8 %all-to-all-start.2 = ((bf16[32,32,8,128]{3,2,1,0:T(8,128)(2,1)}), bf16[32,32,8,128]{3,2,1,0:T(8,128)(2,1)S(1)}, u32[]{:S(2)}, u32[]{:S(2)}) async-start(bf16[32,32,8,128]{3,2,1,0:T(8,128)(2,1)} %middle_back.1), calls=%async_computation.2 | async-start | bytes 4194304 | tf_op jit(solution)/shard_map/all_to_all | solution.py:306
  115.5 1.3 copy-start.1
  116.9 33.5 %all-to-all-start.3 = ((bf16[32,32,8,128]{3,2,1,0:T(8,128)(2,1)}), bf16[32,32,8,128]{3,2,1,0:T(8,128)(2,1)}, u32[]{:S(2)}, u32[]{:S(2)}) async-start(bf16[32,32,8,128]{3,2,1,0:T(8,128)(2,1)} %get-tuple-element.28), calls=%async_computation.3 | async-start | bytes 4194304 | tf_op jit(solution)/shard_map/all_to_all | solution.py:306
  140.1 3.7 %collective-permute-start = (bf16[64,8,8,128]{3,2,1,0:T(8,128)(2,1)S(1)}, bf16[64,8,8,128]{3,2,1,0:T(8,128)(2,1)S(1)}, u32[]{:S(2)}, u32[]{:S(2)}) collective-permute-start(bf16[64,8,8,128]{3,2,1,0:T(8,128)(2,1)S(1)} %slice.3), channel_id=1, source_target_pairs={{0,1},{1,0},{2,3},{3,2},{4,5},{5,4},{6,7},{7,6},{8,9},{9,8},{10,11... | collective-permute-start | bytes 3145736 | tf_op jit(solution)/shard_map/ppermute | solution.py:326
  143.8 1.0 copy-start.4
  202.7 6.4 %copy-start.2 = (bf16[64,9,8,128]{3,2,1,0:T(8,128)(2,1)}, bf16[64,9,8,128]{3,2,1,0:T(8,128)(2,1)S(1)}, u32[]{:S(2)}) copy-start(bf16[64,9,8,128]{3,2,1,0:T(8,128)(2,1)S(1)} %all_to_all.31.mine_ref) | copy-start | bytes 3538948
  202.7 6.4 %collective-permute-start.1 = (bf16[64,9,8,128]{3,2,1,0:T(8,128)(2,1)S(1)}, bf16[64,9,8,128]{3,2,1,0:T(8,128)(2,1)S(1)}, u32[]{:S(2)}, u32[]{:S(2)}) collective-permute-start(bf16[64,9,8,128]{3,2,1,0:T(8,128)(2,1)S(1)} %all_to_all.31.mine_ref), channel_id=1, source_target_pairs={{0,1},{1,0},{2,3},{3,2},{4,5},{5,4},{6,7},{7,6},{8,9},{9,8},{10,11... | collective-permute-start | bytes 3538952 | tf_op jit(solution)/shard_map/ppermute | solution.py:332
  209.1 1.1 copy-start.3

commit v2 on v1

v2 whole, which is shorter than its diff:
```python
import jax
import jax.numpy as jnp
from jax import lax
from jax.experimental import pallas as pl
from jax.experimental.pallas import tpu as pltpu
from jax.sharding import PartitionSpec as P

BF = jnp.bfloat16
F32 = jnp.float32
LANES = 128


def gates(g):
    sig = jax.nn.sigmoid(g)
    return g * sig, sig * (1.0 + g * (1.0 - sig))


def front(x, g, w_first, tj):
    lb, block, width = x.shape

    def body(x_ref, g_ref, w_ref, hid_ref, first_ref, wide, turn):
        @pl.when(pl.program_id(0) == 0)
        def _():
            for i in range(lb):
                wide[:, i * width : (i + 1) * width] = x_ref[i]

        res = jnp.dot(w_ref[...], wide[...], preferred_element_type=F32)
        for i in range(lb):
            part = res[:, i * width : (i + 1) * width]
            first_ref[i] = part
            act, _ = gates(g_ref[i].astype(F32))
            turn[pl.ds(i, tj, stride=lb), :] = part * act
        hid_ref[...] = turn[...].reshape(tj, lb, width).astype(BF)

    return pl.pallas_call(
        body,
        grid=(block // tj,),
        in_specs=[
            pl.BlockSpec((lb, block, width), lambda j: (0, 0, 0)),
            pl.BlockSpec((lb, tj, width), lambda j: (0, j, 0)),
            pl.BlockSpec((tj, block), lambda j: (j, 0)),
        ],
        out_specs=[
            pl.BlockSpec((tj, lb, width), lambda j: (j, 0, 0)),
            pl.BlockSpec((lb, tj, width), lambda j: (0, j, 0)),
        ],
        out_shape=[
            jax.ShapeDtypeStruct((block, lb, width), BF),
            jax.ShapeDtypeStruct((lb, block, width), F32),
        ],
        scratch_shapes=[
            pltpu.VMEM((block, lb * width), BF),
            pltpu.VMEM((tj * lb, width), F32),
        ],
        name="front",
    )(x, g, w_first)


def columns(ref, j, rows):
    return ref[:, j].astype(F32).reshape(rows, LANES).astype(BF)


def middle(x_t, w, tj):
    seq, jp, lb, width = x_t.shape
    nb = seq * lb

    def body(x_ref, w_ref, out_ref):
        for j in range(0, tj, 2):
            pair = jnp.concatenate([columns(x_ref, j, nb), columns(x_ref, j + 1, nb)], axis=1)
            res = jnp.dot(w_ref[...], pair, preferred_element_type=F32)
            for k in range(2):
                part = res[:, k * width : (k + 1) * width]
                out_ref[:, j + k] = part.reshape(seq, lb, width).astype(BF)

    block = pl.BlockSpec((seq, tj, lb, width), lambda j: (0, j, 0, 0))
    return pl.pallas_call(
        body,
        grid=(jp // tj,),
        in_specs=[block, pl.BlockSpec((nb, nb), lambda j: (0, 0))],
        out_specs=block,
        out_shape=jax.ShapeDtypeStruct(x_t.shape, BF),
    )(x_t, w)


def sums(hid_t, cot_t, parts, tj):
    seq, jp, lb, width = cot_t.shape
    nb = seq * lb
    steps = jp // tj
    plane, tiles = parts[0].shape[:2]
    lane_tiles = nb // LANES
    extra = nb // 8 * lane_tiles // plane

    def body(hid_ref, cot_ref, *refs):
        part_refs, out_ref, acc = refs[:-2], refs[-2], refs[-1]
        step = pl.program_id(0)
        total = jnp.zeros((nb, nb), F32)
        for j in range(0, tj, 2):
            hids = jnp.concatenate([columns(hid_ref, j, nb), columns(hid_ref, j + 1, nb)], axis=1)
            cots = jnp.concatenate([columns(cot_ref, j, nb), columns(cot_ref, j + 1, nb)], axis=1)
            total += lax.dot_general(
                cots, hids, (((1,), (1,)), ((), ())), preferred_element_type=F32
            )

        @pl.when(step == 0)
        def _():
            acc[...] = total
            main = part_refs[0][...].astype(F32)
            for ref in part_refs[1:]:
                main += ref[...].astype(F32)
            out_ref[:, :tiles] = main.astype(BF)

        @pl.when(step > 0)
        def _():
            acc[...] += total

        @pl.when(step == steps - 1)
        def _():
            for p in range(plane * extra):
                row, lane = divmod(p, lane_tiles)
                out_ref[p // extra, tiles + p % extra] = acc[
                    row * 8 : row * 8 + 8, lane * LANES : (lane + 1) * LANES
                ].astype(BF)

    block = pl.BlockSpec((seq, tj, lb, width), lambda j: (0, j, 0, 0))
    whole = pl.BlockSpec(parts[0].shape, lambda j: (0, 0, 0, 0))
    shape = (plane, tiles + extra, 8, LANES)
    return pl.pallas_call(
        body,
        grid=(steps,),
        in_specs=[block, block] + [whole] * len(parts),
        out_specs=pl.BlockSpec(shape, lambda j: (0, 0, 0, 0)),
        out_shape=jax.ShapeDtypeStruct(shape, BF),
        scratch_shapes=[pltpu.VMEM((nb, nb), F32)],
        name="sums",
    )(hid_t, cot_t, *parts)


def pack(x, tj):
    lb, block, width = x.shape

    def body(x_ref, out_ref, turn):
        for i in range(lb):
            turn[pl.ds(i, tj, stride=lb), :] = x_ref[i].astype(F32)
        out_ref[...] = turn[...].reshape(tj, lb, width).astype(BF)

    return pl.pallas_call(
        body,
        grid=(block // tj,),
        in_specs=[pl.BlockSpec((lb, tj, width), lambda j: (0, j, 0))],
        out_specs=pl.BlockSpec((tj, lb, width), lambda j: (j, 0, 0)),
        out_shape=jax.ShapeDtypeStruct((block, lb, width), BF),
        scratch_shapes=[pltpu.VMEM((tj * lb, width), F32)],
        name="pack",
    )(x)


def unfold(x, tj):
    block, lb, width = x.shape

    def body(x_ref, out_ref, turn):
        turn[...] = x_ref[...].astype(F32).reshape(tj * lb, width)
        for i in range(lb):
            out_ref[i] = turn[pl.ds(i, tj, stride=lb), :].astype(BF)

    return pl.pallas_call(
        body,
        grid=(block // tj,),
        in_specs=[pl.BlockSpec((tj, lb, width), lambda j: (j, 0, 0))],
        out_specs=pl.BlockSpec((lb, tj, width), lambda j: (0, j, 0)),
        out_shape=jax.ShapeDtypeStruct((lb, block, width), BF),
        scratch_shapes=[pltpu.VMEM((tj * lb, width), F32)],
        name="unfold",
    )(x)


def back(where, gh, first, x, g, tj):
    lb, block, width = x.shape
    steps = block // tj
    half = steps // 2
    tiles = block // LANES

    def body(where_ref, gh_ref, first_ref, x_ref, g_ref, gate_ref, gfa_ref, give_ref, own_ref,
             wide, turn):
        step = pl.program_id(0)

        @pl.when(step == 0)
        def _():
            for i in range(lb):
                wide[:, i * width : (i + 1) * width] = x_ref[i]

        turn[...] = gh_ref[...].astype(F32).reshape(tj * lb, width)
        for i in range(lb):
            gh_i = turn[pl.ds(i, tj, stride=lb), :]
            act, slope = gates(g_ref[i].astype(F32))
            gfa_ref[:, i * width : (i + 1) * width] = (gh_i * act).astype(BF)
            gate_ref[i] = (gh_i * first_ref[i] * slope).astype(BF)
        term = lax.dot_general(
            gfa_ref[...], wide[...], (((1,), (1,)), ((), ())), preferred_element_type=F32
        )

        def store(ref):
            for k in range(tiles):
                part = term[:, k * LANES : (k + 1) * LANES]
                ref[:, k] = part.reshape(tj // 8, 8, LANES).astype(BF)

        @pl.when(step < half)
        def _():
            store(give_ref)

        @pl.when(step >= half)
        def _():
            store(own_ref)

    def at(j, where_ref):
        return (j + (1 - where_ref[0]) * half) % steps

    piece = (tj // 8, tiles, 8, LANES)
    grid_spec = pltpu.PrefetchScalarGridSpec(
        num_scalar_prefetch=1,
        grid=(steps,),
        in_specs=[
            pl.BlockSpec((tj, lb, width), lambda j, c: (at(j, c), 0, 0)),
            pl.BlockSpec((lb, tj, width), lambda j, c: (0, at(j, c), 0)),
            pl.BlockSpec((lb, block, width), lambda j, c: (0, 0, 0)),
            pl.BlockSpec((lb, tj, width), lambda j, c: (0, at(j, c), 0)),
        ],
        out_specs=[
            pl.BlockSpec((lb, tj, width), lambda j, c: (0, at(j, c), 0)),
            pl.BlockSpec((tj, lb * width), lambda j, c: (at(j, c), 0)),
            pl.BlockSpec(piece, lambda j, c: (jnp.minimum(j, half - 1), 0, 0, 0)),
            pl.BlockSpec(piece, lambda j, c: (jnp.maximum(j - half, 0), 0, 0, 0)),
        ],
        scratch_shapes=[
            pltpu.VMEM((block, lb * width), BF),
            pltpu.VMEM((tj * lb, width), F32),
        ],
    )
    half_shape = (block // 16, tiles, 8, LANES)
    return pl.pallas_call(
        body,
        grid_spec=grid_spec,
        out_shape=[
            jax.ShapeDtypeStruct((lb, block, width), BF),
            jax.ShapeDtypeStruct((block, lb * width), BF),
            jax.ShapeDtypeStruct(half_shape, BF),
            jax.ShapeDtypeStruct(half_shape, BF),
        ],
        name="back",
    )(where, gh, first, x, g)


def back_tokens(gfa, w_first, width):
    block, wide = gfa.shape
    lb = wide // width

    def body(gfa_ref, w_ref, out_ref):
        res = lax.dot_general(
            w_ref[...], gfa_ref[...], (((0,), (0,)), ((), ())), preferred_element_type=F32
        )
        out_ref[0] = res[:, :width].astype(BF)
        out_ref[1] = res[:, width:].astype(BF)

    return pl.pallas_call(
        body,
        grid=(lb // 2,),
        in_specs=[
            pl.BlockSpec((block, 2 * width), lambda i: (0, i)),
            pl.BlockSpec((block, block), lambda i: (0, 0)),
        ],
        out_specs=pl.BlockSpec((2, block, width), lambda i: (i, 0, 0)),
        out_shape=jax.ShapeDtypeStruct((lb, block, width), BF),
        name="back_tokens",
    )(gfa, w_first)


def pair_sum(where, own, taken, ring):
    chips, tiles = own.shape[:2]
    step = chips // ring

    def body(where_ref, own_ref, taken_ref, *outs):
        for d in range(ring):
            at = pl.ds(((where_ref[1] + d) % ring) * step, step)
            outs[d][...] = (own_ref[at].astype(F32) + taken_ref[at].astype(F32)).astype(BF)

    vm = pl.BlockSpec(memory_space=pltpu.VMEM)
    return pl.pallas_call(
        body,
        in_specs=[pl.BlockSpec(memory_space=pltpu.SMEM), vm, vm],
        out_specs=[vm] * ring,
        out_shape=[jax.ShapeDtypeStruct((step, tiles, 8, LANES), BF)] * ring,
        name="pair_sum",
    )(where, own, taken)


def plane_sum(parts):
    def body(in_ref, out_ref):
        out_ref[0] = jnp.sum(in_ref[...].astype(F32), axis=0).astype(BF)

    return pl.pallas_call(
        body, out_shape=jax.ShapeDtypeStruct((1,) + parts.shape[1:], BF), name="plane_sum"
    )(parts)


def z_sum(got, tiles):
    ring = len(got)
    extra = got[0].shape[1] - tiles

    def body(*refs):
        out_ref = refs[-1]
        total = jnp.zeros((extra, 8, LANES), F32)
        for d in range(ring):
            out_ref[0, d * tiles : (d + 1) * tiles] = refs[d][0, :tiles]
            total += refs[d][0, tiles:].astype(F32)
        out_ref[0, ring * tiles :] = total.astype(BF)

    return pl.pallas_call(
        body,
        out_shape=jax.ShapeDtypeStruct((1, ring * tiles + extra, 8, LANES), BF),
        name="z_sum",
    )(*got)


def unpack(where, mine, other, block, nb, tiles, scale_first, scale_second):
    ring = len(mine)
    lane_tiles = nb // LANES
    extra = mine[0].shape[1] - ring * tiles
    plane = ring * ring

    def body(where_ref, *refs):
        mine_refs, other_refs = refs[:ring], refs[ring : 2 * ring]
        first_ref, second_ref, both = refs[2 * ring :]
        core, z, y, x = (where_ref[k] for k in range(4))
        for dy in range(ring):
            for dx in range(ring):
                spot = ((y - dy + ring) % ring) * ring + (x - dx + ring) % ring
                for dz in range(ring):
                    chip = ((z - dz + ring) % ring) * plane + spot
                    for ref, c in ((mine_refs[dy], core), (other_refs[dy], 1 - core)):
                        row = pl.multiple_of(c * (block // 2) + chip * 8, 8)
                        for k in range(tiles):
                            first_ref[pl.ds(row, 8), k * LANES : (k + 1) * LANES] = (
                                ref[dx, dz * tiles + k].astype(F32) * scale_first
                            )
                total = mine_refs[dy][dx, ring * tiles :].astype(F32)
                total += other_refs[dy][dx, ring * tiles :].astype(F32)
                both[pl.ds(spot * extra, extra)] = total * scale_second
        for p in range(plane * extra):
            row, lane = divmod(p, lane_tiles)
            second_ref[row * 8 : row * 8 + 8, lane * LANES : (lane + 1) * LANES] = both[p]

    vm = pl.BlockSpec(memory_space=pltpu.VMEM)
    return pl.pallas_call(
        body,
        in_specs=[pl.BlockSpec(memory_space=pltpu.SMEM)] + [vm] * (2 * ring),
        out_specs=[vm, vm],
        out_shape=[
            jax.ShapeDtypeStruct((block, block), F32),
            jax.ShapeDtypeStruct((nb, nb), F32),
        ],
        scratch_shapes=[pltpu.VMEM((plane * extra, 8, LANES), F32)],
        name="unpack",
    )(where, *mine, *other)


def local(tokens, gate, cotangent, w_first, w_second):
    seq_count = lax.axis_size("seq")
    chan_count = lax.axis_size("ch")
    width = tokens.shape[1]
    block = w_first.shape[0]
    lb = tokens.shape[0] // block
    nb = lb * seq_count
    jp = block // seq_count
    rows = lb * block
    ring = 4
    plane = ring * ring
    seq_at, ch_at = lax.axis_index("seq"), lax.axis_index("ch")
    where = jnp.stack([
        ch_at % 2, seq_at // plane * 2 + ch_at // 2, seq_at // ring % ring, seq_at % ring
    ]).astype(jnp.int32)

    def device(core, z, y, x):
        return ((z // 2 * plane + y * ring + x) * 2 + z % 2) * 2 + core

    every = [(c, z, y, x) for c in range(2) for z in range(ring) for y in range(ring)
             for x in range(ring)]

    def shift(value, axis, d):
        pairs = []
        for at in every:
            to = list(at)
            to[axis] = (to[axis] + d) % (ring if axis else 2)
            pairs.append((device(*at), device(*to)))
        return lax.ppermute(value, ("seq", "ch"), pairs)

    planes = [[device(c, z, y, x) for y in range(ring) for x in range(ring)]
              for c in range(2) for z in range(ring)]

    def exchange(x):
        return lax.all_to_all(x, "seq", split_axis=0, concat_axis=0, tiled=True)

    def ring_gather(value, axis):
        return [value] + [shift(value, axis, d) for d in range(1, ring)]

    x = tokens.reshape(lb, block, width)
    g = gate.reshape(lb, block, width)
    cot = pack(cotangent.reshape(lb, block, width), 256)
    cot_t = exchange(cot.reshape(seq_count, jp, lb, width))
    hidden, first = front(x, g, w_first, 256)
    gh_t = middle(cot_t, w_second.T, 8)
    gh_r = exchange(gh_t).reshape(block, lb, width)
    hidden, gh_r = lax.optimization_barrier((hidden, gh_r))
    hid_t = exchange(hidden.reshape(seq_count, jp, lb, width))
    grad_gate, gfa, give, own = back(where, gh_r, first, x, g, 256)
    tiles = own.shape[1]
    taken = shift(give, 0, 1)
    parts = pair_sum(where, own, taken, ring)
    parts = [parts[0]] + [shift(parts[d], 1, d) for d in range(1, ring)]
    part = sums(hid_t, cot_t, parts, 8)
    part = lax.all_to_all(
        part, ("seq", "ch"), 0, 0, tiled=True, axis_index_groups=planes
    )
    mixed_t = middle(hid_t, w_second, 8)
    grad_tokens = back_tokens(gfa, w_first, width)
    mixed_t, part = lax.optimization_barrier((mixed_t, part))
    mixed_r = exchange(mixed_t).reshape(block, lb, width)
    mine = z_sum(ring_gather(plane_sum(part), 1), tiles)
    mine = jnp.concatenate(ring_gather(mine, 3))
    mine = ring_gather(mine, 2)
    other = [shift(value, 0, 1) for value in mine]
    total_width = width * chan_count
    grad_first, grad_second = unpack(
        where, mine, other, block, nb, tiles,
        (nb * total_width) ** -0.5, (block * total_width) ** -0.5,
    )
    mixed = unfold(mixed_r, 256).reshape(rows, width)
    return mixed, grad_tokens.reshape(rows, width), grad_gate.reshape(rows, width), grad_first, grad_second


def solution(mesh):
    return jax.shard_map(
        local,
        mesh=mesh,
        in_specs=(P("seq", "ch"), P("seq", "ch"), P("seq", "ch"), P(), P()),
        out_specs=(P("seq", "ch"), P("seq", "ch"), P("seq", "ch"), P(), P()),
        check_vma=False,
    )
```

time: 219 us -> 232 us (1.059)
  blocking collectives: 49.8 us -> 0 us
  starting transfers between devices: 33.7 us -> 66.6 us
  waiting for transfers between devices: 68.8 us -> 95.3 us
  Pallas kernels: 48.8 us -> 57.3 us
  local copies, waits for them, and re-layouts: 15.2 us -> 9.16 us
    all_to_all x2 -> x0, blocking collectives: 49.8 us -> none  [chip_exchange(): lax.all_to_all(x, ('seq', 'ch'), 0, 0, tiled=True, axis_index_groups=same...]
    ppermute x2 -> x17, waiting for transfers between devices: 2.29 us -> 42.8 us  [shift(): return lax.ppermute(value, ('seq', 'ch'), pairs)]
    ppermute x2 -> x17, starting transfers between devices: 4.59 us -> 31.9 us  [shift(): return lax.ppermute(value, ('seq', 'ch'), pairs)]
    all_to_all x4, waiting for transfers between devices: 66.5 us -> 47.4 us  [exchange(): return lax.all_to_all(x, 'seq', split_axis=0, concat_axis=0, tiled=True)]
    pallas_call x5 -> x10, Pallas kernels: 22.6 us -> 38.2 us  [the longest x2 8.71 us: middle(): pl.pallas_call(body, grid=(jp // tj,), in_specs=[block, pl.BlockSpec((nb,...]
    all_to_all x0 -> x1, starting transfers between devices: none -> 6.86 us  [local(): lax.all_to_all(part, ('seq', 'ch'), 0, 0, tiled=True, axis_index_groups=p...]
    reshape x1 -> x0, local copies, waits for them, and re-layouts: 5.34 us -> none  [local(): cot = cotangent.reshape(lb, seq_count, jp, width).transpose(1, 2, 0, 3)]
    pallas_call x1, Pallas kernels: 16.2 us -> 11 us  [back(): pl.pallas_call(body, grid_spec=grid_spec, out_shape=[jax.ShapeDtypeStruct...]
  transfers between devices with their start and end apart: 6 -> 22, of which waited for: 5 -> 12; matrix products, arithmetic and copies ran while one was open for 2% -> 1% of each run, Pallas kernels for 18% -> 17%
where the time goes in v2:
time: 232 us; the launch traced here: 231 us
  waiting for transfers between devices  95.3 us (41%)
  starting transfers between devices  66.6 us (29%)
  Pallas kernels  57.3 us (25%)
  local copies, waits for them, and re-layouts  9.16 us (4%)
    all_to_all x4, waiting for transfers between devices, exchange(): return lax.all_to_all(x, 'seq', split_axis=0, concat_axis=0, tiled=True)  47.4 us
    ppermute x17, waiting for transfers between devices, shift(): return lax.ppermute(value, ('seq', 'ch'), pairs)  42.8 us
    ppermute x17, starting transfers between devices, shift(): return lax.ppermute(value, ('seq', 'ch'), pairs)  31.9 us
    all_to_all x4, starting transfers between devices, exchange(): return lax.all_to_all(x, 'seq', split_axis=0, concat_axis=0, tiled=True)  27.8 us
    pallas_call x1, Pallas kernels, back(): pl.pallas_call(body, grid_spec=grid_spec, out_shape=[jax.ShapeDtypeStruct...  11 us
    unnamed x35, local copies, waits for them, and re-layouts  9.16 us
    pallas_call x2, Pallas kernels, middle(): pl.pallas_call(body, grid=(jp // tj,), in_specs=[block, pl.BlockSpec((nb,...  8.71 us
    pallas_call x1, Pallas kernels, front(): pl.pallas_call(body, grid=(block // tj,), in_specs=[pl.BlockSpec((lb, blo...  8.2 us
  transfers between devices with their start and end apart: 22, of which 12 were waited for; matrix products, arithmetic and copies ran while one was open for 1% of the time, Pallas kernels for 17%

profile of v2, /device:TPU:1, one launch (start us, length us, event | category | flops | bytes accessed | tf_op | source)
XLA Modules:
  0.0 230.7 jit_solution(17892990751169808468)
XLA Ops:
  0.6 4.4 %pack.1 = bf16[1024,8,128]{2,1,0:T(8,128)(2,1)} custom-call(bf16[8,1024,128]{2,1,0:T(8,128)(2,1)} %bitcast.23), custom_call_target="tpu_custom_call" | custom-call | tf_op jit(solution)/shard_map/pack/pallas_call | solution.py:146
  5.0 11.3 %all-to-all-start = ((bf16[32,32,8,128]{3,2,1,0:T(8,128)(2,1)}), bf16[32,32,8,128]{3,2,1,0:T(8,128)(2,1)S(1)}, u32[]{:S(2)}, u32[]{:S(2)}) async-start(bf16[32,32,8,128]{3,2,1,0:T(8,128)(2,1)} %bitcast.20), calls=%async_computation | async-start | bytes 4194304 | tf_op jit(solution)/shard_map/all_to_all | solution.py:399
  17.1 27.6 %all-to-all-done.x_ref.cot_ref = bf16[32,32,8,128]{3,2,1,0:T(8,128)(2,1)S(1)} async-done(((bf16[32,32,8,128]{3,2,1,0:T(8,128)(2,1)}), bf16[32,32,8,128]{3,2,1,0:T(8,128)(2,1)S(1)}, u32[]{:S(2)}, u32[]{:S(2)}) %all-to-all-start) | async-done | bytes 2097184 | tf_op jit(solution)/shard_map/all_to_all | solution.py:399
  46.1 4.3 %shard_map.92 = bf16[32,32,8,128]{3,2,1,0:T(8,128)(2,1)} custom-call(bf16[32,32,8,128]{3,2,1,0:T(8,128)(2,1)} %copy-done, bf16[256,256]{1,0:T(8,128)(2,1)} %bitcast.26), custom_call_target="tpu_custom_call" | custom-call | tf_op jit(solution)/shard_map/pallas_call | solution.py:76
  50.4 5.8 %all-to-all-start.1 = ((bf16[32,32,8,128]{3,2,1,0:T(8,128)(2,1)}), bf16[32,32,8,128]{3,2,1,0:T(8,128)(2,1)S(1)}, u32[]{:S(2)}, u32[]{:S(2)}) async-start(bf16[32,32,8,128]{3,2,1,0:T(8,128)(2,1)} %shard_map.92), calls=%async_computation.1 | async-start | bytes 4194304 | tf_op jit(solution)/shard_map/all_to_all | solution.py:399
  56.2 8.2 %front.1 = (bf16[1024,8,128]{2,1,0:T(8,128)(2,1)}, f32[8,1024,128]{2,1,0:T(8,128)}) custom-call(bf16[8,1024,128]{2,1,0:T(8,128)(2,1)} %bitcast.15, bf16[8,1024,128]{2,1,0:T(8,128)(2,1)} %bitcast.17, bf16[1024,1024]{1,0:T(8,128)(2,1)} %w_ref.5), custom_call_target="tpu_custom_call" | custom-call | tf_op jit(solution)/shard_map/front/pallas_call | solution.py:35
  64.4 19.7 %all-to-all-done.1 = bf16[32,32,8,128]{3,2,1,0:T(8,128)(2,1)S(1)} async-done(((bf16[32,32,8,128]{3,2,1,0:T(8,128)(2,1)}), bf16[32,32,8,128]{3,2,1,0:T(8,128)(2,1)S(1)}, u32[]{:S(2)}, u32[]{:S(2)}) %all-to-all-start.1) | async-done | bytes 2097184 | tf_op jit(solution)/shard_map/all_to_all | solution.py:399
  85.5 6.3 %all-to-all-start.2 = ((bf16[32,32,8,128]{3,2,1,0:T(8,128)(2,1)}), bf16[32,32,8,128]{3,2,1,0:T(8,128)(2,1)S(1)}, u32[]{:S(2)}, u32[]{:S(2)}) async-start(bf16[32,32,8,128]{3,2,1,0:T(8,128)(2,1)} %bitcast.24), calls=%async_computation.2 | async-start | bytes 4194304 | tf_op jit(solution)/shard_map/all_to_all | solution.py:399
  92.5 11.0 %back.1 = (bf16[8,1024,128]{2,1,0:T(8,128)(2,1)}, bf16[1024,1024]{1,0:T(8,128)(2,1)}, bf16[64,8,8,128]{3,2,1,0:T(8,128)(2,1)}, bf16[64,8,8,128]{3,2,1,0:T(8,128)(2,1)}) custom-call(s32[4]{0:T(128)} %pad_add_fusion.where_ref, bf16[1024,8,128]{2,1,0:T(8,128)(2,1)} %bitcast.21, f32[8,1024,128]{2,1,0:T(8,128)} %get-tuple-element.24.first_ref, ...), custom_call_target="tpu_custom_call" | custom-call | tf_op jit(solution)/shard_map/back/pallas_call | solution.py:239
  104.2 2.5 %collective-permute-done.taken_ref = bf16[64,8,8,128]{3,2,1,0:T(8,128)(2,1)S(1)} collective-permute-done((bf16[64,8,8,128]{3,2,1,0:T(8,128)(2,1)}, bf16[64,8,8,128]{3,2,1,0:T(8,128)(2,1)S(1)}, u32[]{:S(2)}, u32[]{:S(2)}) %collective-permute-start) | collective-permute-done | bytes 1048608 | tf_op jit(solution)/shard_map/ppermute | solution.py:393
  107.7 2.7 %pair_sum.1 = (bf16[16,8,8,128]{3,2,1,0:T(8,128)(2,1)}, bf16[16,8,8,128]{3,2,1,0:T(8,128)(2,1)}, bf16[16,8,8,128]{3,2,1,0:T(8,128)(2,1)}, bf16[16,8,8,128]{3,2,1,0:T(8,128)(2,1)}) custom-call(s32[4]{0:T(128)} %pad_add_fusion.where_ref, bf16[64,8,8,128]{3,2,1,0:T(8,128)(2,1)} %get-tuple-element.25.own_ref, bf16[64,8,8,128]{3,2,1,0:T(8,128)(2,1)} %copy-done.6), custom_call_target="tpu_custom_call" | custom-call | tf_op jit(solution)/shard_map/pair_sum/pallas_call | solution.py:286
  111.2 3.6 %collective-permute-start.2 = (bf16[16,8,8,128]{3,2,1,0:T(8,128)(2,1)}, bf16[16,8,8,128]{3,2,1,0:T(8,128)(2,1)S(1)}, u32[]{:S(2)}, u32[]{:S(2)}) collective-permute-start(bf16[16,8,8,128]{3,2,1,0:T(8,128)(2,1)} %get-tuple-element.29), channel_id=1, source_target_pairs={{0,64},{4,68},{8,72},{12,76},{16,80},{20,84},{24,88},{28,92},{32,9... | collective-permute-start | bytes 786440 | tf_op jit(solution)/shard_map/ppermute | solution.py:393
  115.5 9.7 %collective-permute-done.1.refs_1_ = bf16[16,8,8,128]{3,2,1,0:T(8,128)(2,1)S(1)} collective-permute-done((bf16[16,8,8,128]{3,2,1,0:T(8,128)(2,1)}, bf16[16,8,8,128]{3,2,1,0:T(8,128)(2,1)S(1)}, u32[]{:S(2)}, u32[]{:S(2)}) %collective-permute-start.1) | collective-permute-done | bytes 262176 | tf_op jit(solution)/shard_map/ppermute | solution.py:393
  125.3 5.3 %collective-permute-done.2.refs_2_ = bf16[16,8,8,128]{3,2,1,0:T(8,128)(2,1)S(1)} collective-permute-done((bf16[16,8,8,128]{3,2,1,0:T(8,128)(2,1)}, bf16[16,8,8,128]{3,2,1,0:T(8,128)(2,1)S(1)}, u32[]{:S(2)}, u32[]{:S(2)}) %collective-permute-start.2) | collective-permute-done | bytes 262176 | tf_op jit(solution)/shard_map/ppermute | solution.py:393
  132.1 4.8 %sums.1 = bf16[16,12,8,128]{3,2,1,0:T(8,128)(2,1)} custom-call(bf16[32,32,8,128]{3,2,1,0:T(8,128)(2,1)} %copy-done.1, bf16[32,32,8,128]{3,2,1,0:T(8,128)(2,1)} %copy-done, bf16[16,8,8,128]{3,2,1,0:T(8,128)(2,1)} %get-tuple-element.27.refs_0_, bf16[16,8,8,128]{3,2,1,0:T(8,128)(2,1)} %copy-done.11, bf16[16,8,8,128]{3,2,1,0:T(8,128)(2,1)} %copy-done.12, ...), custom_call_target="tpu_custom_call" | custom-call | tf_op jit(solution)/shard_map/sums/pallas_call | solution.py:127
  136.9 6.9 %all-to-all-start.3 = ((bf16[16,12,8,128]{3,2,1,0:T(8,128)(2,1)}), bf16[16,12,8,128]{3,2,1,0:T(8,128)(2,1)S(1)}, u32[]{:S(2)}, u32[]{:S(2)}) async-start(bf16[16,12,8,128]{3,2,1,0:T(8,128)(2,1)} %sums.1), calls=%async_computation.3 | async-start | bytes 786432 | tf_op jit(solution)/shard_map/all_to_all | solution.py:419
  143.8 4.4 %shard_map.93 = bf16[32,32,8,128]{3,2,1,0:T(8,128)(2,1)} custom-call(bf16[32,32,8,128]{3,2,1,0:T(8,128)(2,1)} %copy-done.1, bf16[256,256]{1,0:T(8,128)(2,1)} %w_ref.4), custom_call_target="tpu_custom_call" | custom-call | tf_op jit(solution)/shard_map/pallas_call | solution.py:76
  148.1 5.1 %all-to-all-done.3.in_ref = bf16[16,12,8,128]{3,2,1,0:T(8,128)(2,1)S(1)} async-done(((bf16[16,12,8,128]{3,2,1,0:T(8,128)(2,1)}), bf16[16,12,8,128]{3,2,1,0:T(8,128)(2,1)S(1)}, u32[]{:S(2)}, u32[]{:S(2)}) %all-to-all-start.3) | async-done | bytes 393248 | tf_op jit(solution)/shard_map/all_to_all | solution.py:419
  154.0 4.4 %all-to-all-start.4 = ((bf16[32,32,8,128]{3,2,1,0:T(8,128)(2,1)}), bf16[32,32,8,128]{3,2,1,0:T(8,128)(2,1)S(1)}, u32[]{:S(2)}, u32[]{:S(2)}) async-start(bf16[32,32,8,128]{3,2,1,0:T(8,128)(2,1)} %shard_map.93), calls=%async_computation.4 | async-start | bytes 4194304 | tf_op jit(solution)/shard_map/all_to_all | solution.py:399
  158.4 1.7 plane_sum.1.refs_0_
  160.2 3.3 %collective-permute-start.5 = (bf16[1,12,8,128]{3,2,1,0:T(8,128)(2,1)}, bf16[1,12,8,128]{3,2,1,0:T(8,128)(2,1)S(1)}, u32[]{:S(2)}, u32[]{:S(2)}) collective-permute-start(bf16[1,12,8,128]{3,2,1,0:T(8,128)(2,1)} %plane_sum.1.refs_0_), channel_id=1, source_target_pairs={{0,64},{4,68},{8,72},{12,76},{16,80},{20,84},{24,88},{28,92},{32,9... | collective-permute-start | bytes 73736 | tf_op jit(solution)/shard_map/ppermute | solution.py:393
  164.9 18.9 %collective-permute-done.4.refs_1_ = bf16[1,12,8,128]{3,2,1,0:T(8,128)(2,1)S(1)} collective-permute-done((bf16[1,12,8,128]{3,2,1,0:T(8,128)(2,1)}, bf16[1,12,8,128]{3,2,1,0:T(8,128)(2,1)S(1)}, u32[]{:S(2)}, u32[]{:S(2)}) %collective-permute-start.4) | collective-permute-done | bytes 24608 | tf_op jit(solution)/shard_map/ppermute | solution.py:393
  186.4 3.2 %collective-permute-start.7 = (bf16[1,36,8,128]{3,2,1,0:T(8,128)(2,1)}, bf16[1,36,8,128]{3,2,1,0:T(8,128)(2,1)S(1)}, u32[]{:S(2)}, u32[]{:S(2)}) collective-permute-start(bf16[1,36,8,128]{3,2,1,0:T(8,128)(2,1)} %z_sum.1), channel_id=1, source_target_pairs={{0,4},{4,8},{8,12},{12,0},{16,20},{20,24},{24,28},{28,16},{32,36},... | collective-permute-start | bytes 221192 | tf_op jit(solution)/shard_map/ppermute | solution.py:393
  189.6 2.9 %collective-permute-start.8 = (bf16[1,36,8,128]{3,2,1,0:T(8,128)(2,1)}, bf16[1,36,8,128]{3,2,1,0:T(8,128)(2,1)S(1)}, u32[]{:S(2)}, u32[]{:S(2)}) collective-permute-start(bf16[1,36,8,128]{3,2,1,0:T(8,128)(2,1)} %z_sum.1), channel_id=1, source_target_pairs={{0,8},{4,12},{8,0},{12,4},{16,24},{20,28},{24,16},{28,20},{32,40},... | collective-permute-start | bytes 221192 | tf_op jit(solution)/shard_map/ppermute | solution.py:393
  193.2 2.2 collective-permute-done.8
  197.7 2.4 %collective-permute-start.11 = (bf16[4,36,8,128]{3,2,1,0:T(8,128)(2,1)S(1)}, bf16[4,36,8,128]{3,2,1,0:T(8,128)(2,1)S(1)}, u32[]{:S(2)}, u32[]{:S(2)}) collective-permute-start(bf16[4,36,8,128]{3,2,1,0:T(8,128)(2,1)S(1)} %pad_maximum_fusion.refs_0_), channel_id=1, source_target_pairs={{0,32},{4,36},{8,40},{12,44},{16,48},{20,52},{24,56},{28,60},{32,0... | collective-permute-start | bytes 884744 | tf_op jit(solution)/shard_map/ppermute | solution.py:393
  200.6 3.0 %collective-permute-start.13 = (bf16[4,36,8,128]{3,2,1,0:T(8,128)(2,1)S(1)}, bf16[4,36,8,128]{3,2,1,0:T(8,128)(2,1)}, u32[]{:S(2)}, u32[]{:S(2)}) collective-permute-start(bf16[4,36,8,128]{3,2,1,0:T(8,128)(2,1)S(1)} %pad_maximum_fusion.refs_0_), channel_id=1, source_target_pairs={{0,1},{4,5},{8,9},{12,13},{16,17},{20,21},{24,25},{28,29},{32,33},... | collective-permute-start | bytes 884744 | tf_op jit(solution)/shard_map/ppermute | solution.py:393
  204.8 5.4 %collective-permute-start.14 = (bf16[4,36,8,128]{3,2,1,0:T(8,128)(2,1)S(1)}, bf16[4,36,8,128]{3,2,1,0:T(8,128)(2,1)}, u32[]{:S(2)}, u32[]{:S(2)}) collective-permute-start(bf16[4,36,8,128]{3,2,1,0:T(8,128)(2,1)S(1)} %collective-permute-done.10.refs_1_), channel_id=1, source_target_pairs={{0,1},{4,5},{8,9},{12,13},{16,17},{20,21},{24,25},{28,29},{32,33},... | collective-permute-start | bytes 884744 | tf_op jit(solution)/shard_map/ppermute | solution.py:393
  211.5 2.9 %collective-permute-start.15 = (bf16[4,36,8,128]{3,2,1,0:T(8,128)(2,1)S(1)}, bf16[4,36,8,128]{3,2,1,0:T(8,128)(2,1)}, u32[]{:S(2)}, u32[]{:S(2)}) collective-permute-start(bf16[4,36,8,128]{3,2,1,0:T(8,128)(2,1)S(1)} %collective-permute-done.11.refs_2_), channel_id=1, source_target_pairs={{0,1},{4,5},{8,9},{12,13},{16,17},{20,21},{24,25},{28,29},{32,33},... | collective-permute-start | bytes 884744 | tf_op jit(solution)/shard_map/ppermute | solution.py:393
  214.8 6.2 %back_tokens.1 = bf16[8,1024,128]{2,1,0:T(8,128)(2,1)} custom-call(bf16[1024,1024]{1,0:T(8,128)(2,1)} %get-tuple-element.32.gfa_ref, bf16[1024,1024]{1,0:T(8,128)(2,1)} %w_ref.5), custom_call_target="tpu_custom_call" | custom-call | tf_op jit(solution)/shard_map/back_tokens/pallas_call | solution.py:263
  221.2 4.1 %unpack.1 = (f32[1024,1024]{1,0:T(8,128)}, f32[256,256]{1,0:T(8,128)}) custom-call(s32[4]{0:T(128)} %pad_add_fusion.where_ref, bf16[4,36,8,128]{3,2,1,0:T(8,128)(2,1)} %copy-done.5, bf16[4,36,8,128]{3,2,1,0:T(8,128)(2,1)} %copy-done.8, bf16[4,36,8,128]{3,2,1,0:T(8,128)(2,1)} %copy-done.9, bf16[4,36,8,128]{3,2,1,0:T(8,128)(2,1)} %copy-done.10, ...), custom_call_target="tpu_custom_call" | custom-call | tf_op jit(solution)/shard_map/unpack/pallas_call | solution.py:352
  226.6 4.2 %unfold.1 = bf16[8,1024,128]{2,1,0:T(8,128)(2,1)} custom-call(bf16[1024,8,128]{2,1,0:T(8,128)(2,1)} %bitcast.19), custom_call_target="tpu_custom_call" | custom-call | tf_op jit(solution)/shard_map/unfold/pallas_call | solution.py:165
  (61 shorter events, 21.6 us)
Async XLA Ops:
  5.0 11.3 %copy-start.7 = (bf16[256,256]{1,0:T(8,128)(2,1)S(1)}, bf16[256,256]{1,0:T(8,128)(2,1)}, u32[]{:S(2)}) copy-start(bf16[256,256]{1,0:T(8,128)(2,1)} %w_ref.4) | copy-start | bytes 393220
  5.0 39.7 %all-to-all-start = ((bf16[32,32,8,128]{3,2,1,0:T(8,128)(2,1)}), bf16[32,32,8,128]{3,2,1,0:T(8,128)(2,1)S(1)}, u32[]{:S(2)}, u32[]{:S(2)}) async-start(bf16[32,32,8,128]{3,2,1,0:T(8,128)(2,1)} %bitcast.20), calls=%async_computation | async-start | bytes 4194304 | tf_op jit(solution)/shard_map/all_to_all | solution.py:399
  44.7 1.3 copy-start
  50.4 33.8 %all-to-all-start.1 = ((bf16[32,32,8,128]{3,2,1,0:T(8,128)(2,1)}), bf16[32,32,8,128]{3,2,1,0:T(8,128)(2,1)S(1)}, u32[]{:S(2)}, u32[]{:S(2)}) async-start(bf16[32,32,8,128]{3,2,1,0:T(8,128)(2,1)} %shard_map.92), calls=%async_computation.1 | async-start | bytes 4194304 | tf_op jit(solution)/shard_map/all_to_all | solution.py:399
  84.2 1.3 copy-start.3
  85.5 45.1 %all-to-all-start.2 = ((bf16[32,32,8,128]{3,2,1,0:T(8,128)(2,1)}), bf16[32,32,8,128]{3,2,1,0:T(8,128)(2,1)S(1)}, u32[]{:S(2)}, u32[]{:S(2)}) async-start(bf16[32,32,8,128]{3,2,1,0:T(8,128)(2,1)} %bitcast.24), calls=%async_computation.2 | async-start | bytes 4194304 | tf_op jit(solution)/shard_map/all_to_all | solution.py:399
  103.4 3.3 %collective-permute-start = (bf16[64,8,8,128]{3,2,1,0:T(8,128)(2,1)}, bf16[64,8,8,128]{3,2,1,0:T(8,128)(2,1)S(1)}, u32[]{:S(2)}, u32[]{:S(2)}) collective-permute-start(bf16[64,8,8,128]{3,2,1,0:T(8,128)(2,1)} %get-tuple-element.26), channel_id=1, source_target_pairs={{0,1},{4,5},{8,9},{12,13},{16,17},{20,21},{24,25},{28,29},{32,33},... | collective-permute-start | bytes 3145736 | tf_op jit(solution)/shard_map/ppermute | solution.py:393
  110.4 14.8 %collective-permute-start.1 = (bf16[16,8,8,128]{3,2,1,0:T(8,128)(2,1)}, bf16[16,8,8,128]{3,2,1,0:T(8,128)(2,1)S(1)}, u32[]{:S(2)}, u32[]{:S(2)}) collective-permute-start(bf16[16,8,8,128]{3,2,1,0:T(8,128)(2,1)} %get-tuple-element.28), channel_id=1, source_target_pairs={{0,2},{4,6},{8,10},{12,14},{16,18},{20,22},{24,26},{28,30},{32,34}... | collective-permute-start | bytes 786440 | tf_op jit(solution)/shard_map/ppermute | solution.py:393
  111.2 19.4 %collective-permute-start.2 = (bf16[16,8,8,128]{3,2,1,0:T(8,128)(2,1)}, bf16[16,8,8,128]{3,2,1,0:T(8,128)(2,1)S(1)}, u32[]{:S(2)}, u32[]{:S(2)}) collective-permute-start(bf16[16,8,8,128]{3,2,1,0:T(8,128)(2,1)} %get-tuple-element.29), channel_id=1, source_target_pairs={{0,64},{4,68},{8,72},{12,76},{16,80},{20,84},{24,88},{28,92},{32,9... | collective-permute-start | bytes 786440 | tf_op jit(solution)/shard_map/ppermute | solution.py:393
  114.8 15.8 %collective-permute-start.3 = (bf16[16,8,8,128]{3,2,1,0:T(8,128)(2,1)}, bf16[16,8,8,128]{3,2,1,0:T(8,128)(2,1)S(1)}, u32[]{:S(2)}, u32[]{:S(2)}) collective-permute-start(bf16[16,8,8,128]{3,2,1,0:T(8,128)(2,1)} %get-tuple-element.30), channel_id=1, source_target_pairs={{0,66},{4,70},{8,74},{12,78},{16,82},{20,86},{24,90},{28,94},{32,9... | collective-permute-start | bytes 786440 | tf_op jit(solution)/shard_map/ppermute | solution.py:393
  125.3 5.3 %copy-start.11 = (bf16[16,8,8,128]{3,2,1,0:T(8,128)(2,1)}, bf16[16,8,8,128]{3,2,1,0:T(8,128)(2,1)S(1)}, u32[]{:S(2)}) copy-start(bf16[16,8,8,128]{3,2,1,0:T(8,128)(2,1)S(1)} %collective-permute-done.1.refs_1_) | copy-start | bytes 786436
  130.6 1.5 copy-start.1
  136.9 16.4 %all-to-all-start.3 = ((bf16[16,12,8,128]{3,2,1,0:T(8,128)(2,1)}), bf16[16,12,8,128]{3,2,1,0:T(8,128)(2,1)S(1)}, u32[]{:S(2)}, u32[]{:S(2)}) async-start(bf16[16,12,8,128]{3,2,1,0:T(8,128)(2,1)} %sums.1), calls=%async_computation.3 | async-start | bytes 786432 | tf_op jit(solution)/shard_map/all_to_all | solution.py:419
  154.0 71.2 %all-to-all-start.4 = ((bf16[32,32,8,128]{3,2,1,0:T(8,128)(2,1)}), bf16[32,32,8,128]{3,2,1,0:T(8,128)(2,1)S(1)}, u32[]{:S(2)}, u32[]{:S(2)}) async-start(bf16[32,32,8,128]{3,2,1,0:T(8,128)(2,1)} %shard_map.93), calls=%async_computation.4 | async-start | bytes 4194304 | tf_op jit(solution)/shard_map/all_to_all | solution.py:399
  160.1 23.7 %collective-permute-start.4 = (bf16[1,12,8,128]{3,2,1,0:T(8,128)(2,1)}, bf16[1,12,8,128]{3,2,1,0:T(8,128)(2,1)S(1)}, u32[]{:S(2)}, u32[]{:S(2)}) collective-permute-start(bf16[1,12,8,128]{3,2,1,0:T(8,128)(2,1)} %plane_sum.1.refs_0_), channel_id=1, source_target_pairs={{0,2},{4,6},{8,10},{12,14},{16,18},{20,22},{24,26},{28,30},{32,34}... | collective-permute-start | bytes 73736 | tf_op jit(solution)/shard_map/ppermute | solution.py:393
  160.2 23.6 %collective-permute-start.5 = (bf16[1,12,8,128]{3,2,1,0:T(8,128)(2,1)}, bf16[1,12,8,128]{3,2,1,0:T(8,128)(2,1)S(1)}, u32[]{:S(2)}, u32[]{:S(2)}) collective-permute-start(bf16[1,12,8,128]{3,2,1,0:T(8,128)(2,1)} %plane_sum.1.refs_0_), channel_id=1, source_target_pairs={{0,64},{4,68},{8,72},{12,76},{16,80},{20,84},{24,88},{28,92},{32,9... | collective-permute-start | bytes 73736 | tf_op jit(solution)/shard_map/ppermute | solution.py:393
  163.5 20.3 %collective-permute-start.6 = (bf16[1,12,8,128]{3,2,1,0:T(8,128)(2,1)}, bf16[1,12,8,128]{3,2,1,0:T(8,128)(2,1)S(1)}, u32[]{:S(2)}, u32[]{:S(2)}) collective-permute-start(bf16[1,12,8,128]{3,2,1,0:T(8,128)(2,1)} %plane_sum.1.refs_0_), channel_id=1, source_target_pairs={{0,66},{4,70},{8,74},{12,78},{16,82},{20,86},{24,90},{28,94},{32,9... | collective-permute-start | bytes 73736 | tf_op jit(solution)/shard_map/ppermute | solution.py:393
  186.4 6.8 %collective-permute-start.7 = (bf16[1,36,8,128]{3,2,1,0:T(8,128)(2,1)}, bf16[1,36,8,128]{3,2,1,0:T(8,128)(2,1)S(1)}, u32[]{:S(2)}, u32[]{:S(2)}) collective-permute-start(bf16[1,36,8,128]{3,2,1,0:T(8,128)(2,1)} %z_sum.1), channel_id=1, source_target_pairs={{0,4},{4,8},{8,12},{12,0},{16,20},{20,24},{24,28},{28,16},{32,36},... | collective-permute-start | bytes 221192 | tf_op jit(solution)/shard_map/ppermute | solution.py:393
  189.6 5.8 %collective-permute-start.8 = (bf16[1,36,8,128]{3,2,1,0:T(8,128)(2,1)}, bf16[1,36,8,128]{3,2,1,0:T(8,128)(2,1)S(1)}, u32[]{:S(2)}, u32[]{:S(2)}) collective-permute-start(bf16[1,36,8,128]{3,2,1,0:T(8,128)(2,1)} %z_sum.1), channel_id=1, source_target_pairs={{0,8},{4,12},{8,0},{12,4},{16,24},{20,28},{24,16},{28,20},{32,40},... | collective-permute-start | bytes 221192 | tf_op jit(solution)/shard_map/ppermute | solution.py:393
  192.4 3.8 %collective-permute-start.9 = (bf16[1,36,8,128]{3,2,1,0:T(8,128)(2,1)}, bf16[1,36,8,128]{3,2,1,0:T(8,128)(2,1)S(1)}, u32[]{:S(2)}, u32[]{:S(2)}) collective-permute-start(bf16[1,36,8,128]{3,2,1,0:T(8,128)(2,1)} %z_sum.1), channel_id=1, source_target_pairs={{0,12},{4,0},{8,4},{12,8},{16,28},{20,16},{24,20},{28,24},{32,44},... | collective-permute-start | bytes 221192 | tf_op jit(solution)/shard_map/ppermute | solution.py:393
  197.2 23.9 %copy-start.5 = (bf16[4,36,8,128]{3,2,1,0:T(8,128)(2,1)}, bf16[4,36,8,128]{3,2,1,0:T(8,128)(2,1)S(1)}, u32[]{:S(2)}) copy-start(bf16[4,36,8,128]{3,2,1,0:T(8,128)(2,1)S(1)} %pad_maximum_fusion.refs_0_) | copy-start | bytes 884740
  197.2 7.6 %collective-permute-start.10 = (bf16[4,36,8,128]{3,2,1,0:T(8,128)(2,1)S(1)}, bf16[4,36,8,128]{3,2,1,0:T(8,128)(2,1)S(1)}, u32[]{:S(2)}, u32[]{:S(2)}) collective-permute-start(bf16[4,36,8,128]{3,2,1,0:T(8,128)(2,1)S(1)} %pad_maximum_fusion.refs_0_), channel_id=1, source_target_pairs={{0,16},{4,20},{8,24},{12,28},{16,32},{20,36},{24,40},{28,44},{32,4... | collective-permute-start | bytes 884744 | tf_op jit(solution)/shard_map/ppermute | solution.py:393
  197.7 13.8 %collective-permute-start.11 = (bf16[4,36,8,128]{3,2,1,0:T(8,128)(2,1)S(1)}, bf16[4,36,8,128]{3,2,1,0:T(8,128)(2,1)S(1)}, u32[]{:S(2)}, u32[]{:S(2)}) collective-permute-start(bf16[4,36,8,128]{3,2,1,0:T(8,128)(2,1)S(1)} %pad_maximum_fusion.refs_0_), channel_id=1, source_target_pairs={{0,32},{4,36},{8,40},{12,44},{16,48},{20,52},{24,56},{28,60},{32,0... | collective-permute-start | bytes 884744 | tf_op jit(solution)/shard_map/ppermute | solution.py:393
  200.1 14.3 %collective-permute-start.12 = (bf16[4,36,8,128]{3,2,1,0:T(8,128)(2,1)S(1)}, bf16[4,36,8,128]{3,2,1,0:T(8,128)(2,1)S(1)}, u32[]{:S(2)}, u32[]{:S(2)}) collective-permute-start(bf16[4,36,8,128]{3,2,1,0:T(8,128)(2,1)S(1)} %pad_maximum_fusion.refs_0_), channel_id=1, source_target_pairs={{0,48},{4,52},{8,56},{12,60},{16,0},{20,4},{24,8},{28,12},{32,16},... | collective-permute-start | bytes 884744 | tf_op jit(solution)/shard_map/ppermute | solution.py:393
  200.6 20.5 %collective-permute-start.13 = (bf16[4,36,8,128]{3,2,1,0:T(8,128)(2,1)S(1)}, bf16[4,36,8,128]{3,2,1,0:T(8,128)(2,1)}, u32[]{:S(2)}, u32[]{:S(2)}) collective-permute-start(bf16[4,36,8,128]{3,2,1,0:T(8,128)(2,1)S(1)} %pad_maximum_fusion.refs_0_), channel_id=1, source_target_pairs={{0,1},{4,5},{8,9},{12,13},{16,17},{20,21},{24,25},{28,29},{32,33},... | collective-permute-start | bytes 884744 | tf_op jit(solution)/shard_map/ppermute | solution.py:393
  204.8 16.3 %copy-start.8 = (bf16[4,36,8,128]{3,2,1,0:T(8,128)(2,1)}, bf16[4,36,8,128]{3,2,1,0:T(8,128)(2,1)S(1)}, u32[]{:S(2)}) copy-start(bf16[4,36,8,128]{3,2,1,0:T(8,128)(2,1)S(1)} %collective-permute-done.10.refs_1_) | copy-start | bytes 884740
  204.8 16.3 %collective-permute-start.14 = (bf16[4,36,8,128]{3,2,1,0:T(8,128)(2,1)S(1)}, bf16[4,36,8,128]{3,2,1,0:T(8,128)(2,1)}, u32[]{:S(2)}, u32[]{:S(2)}) collective-permute-start(bf16[4,36,8,128]{3,2,1,0:T(8,128)(2,1)S(1)} %collective-permute-done.10.refs_1_), channel_id=1, source_target_pairs={{0,1},{4,5},{8,9},{12,13},{16,17},{20,21},{24,25},{28,29},{32,33},... | collective-permute-start | bytes 884744 | tf_op jit(solution)/shard_map/ppermute | solution.py:393
  211.5 9.6 %copy-start.9 = (bf16[4,36,8,128]{3,2,1,0:T(8,128)(2,1)}, bf16[4,36,8,128]{3,2,1,0:T(8,128)(2,1)S(1)}, u32[]{:S(2)}) copy-start(bf16[4,36,8,128]{3,2,1,0:T(8,128)(2,1)S(1)} %collective-permute-done.11.refs_2_) | copy-start | bytes 884740
  211.5 9.6 %collective-permute-start.15 = (bf16[4,36,8,128]{3,2,1,0:T(8,128)(2,1)S(1)}, bf16[4,36,8,128]{3,2,1,0:T(8,128)(2,1)}, u32[]{:S(2)}, u32[]{:S(2)}) collective-permute-start(bf16[4,36,8,128]{3,2,1,0:T(8,128)(2,1)S(1)} %collective-permute-done.11.refs_2_), channel_id=1, source_target_pairs={{0,1},{4,5},{8,9},{12,13},{16,17},{20,21},{24,25},{28,29},{32,33},... | collective-permute-start | bytes 884744 | tf_op jit(solution)/shard_map/ppermute | solution.py:393
  214.4 6.7 %copy-start.10 = (bf16[4,36,8,128]{3,2,1,0:T(8,128)(2,1)}, bf16[4,36,8,128]{3,2,1,0:T(8,128)(2,1)S(1)}, u32[]{:S(2)}) copy-start(bf16[4,36,8,128]{3,2,1,0:T(8,128)(2,1)S(1)} %collective-permute-done.12.refs_3_) | copy-start | bytes 884740
  214.4 6.7 %collective-permute-start.16 = (bf16[4,36,8,128]{3,2,1,0:T(8,128)(2,1)S(1)}, bf16[4,36,8,128]{3,2,1,0:T(8,128)(2,1)}, u32[]{:S(2)}, u32[]{:S(2)}) collective-permute-start(bf16[4,36,8,128]{3,2,1,0:T(8,128)(2,1)S(1)} %collective-permute-done.12.refs_3_), channel_id=1, source_target_pairs={{0,1},{4,5},{8,9},{12,13},{16,17},{20,21},{24,25},{28,29},{32,33},... | collective-permute-start | bytes 884744 | tf_op jit(solution)/shard_map/ppermute | solution.py:393
  225.2 1.3 copy-start.2
  (7 other events, 5.0 us)

commit v3 on v2

v3 whole, which is shorter than its diff:
```python
import jax
import jax.numpy as jnp
from jax import lax
from jax.experimental import pallas as pl
from jax.experimental.pallas import tpu as pltpu
from jax.sharding import PartitionSpec as P

BF = jnp.bfloat16
F32 = jnp.float32
LANES = 128
MIB = 1 << 20


def gates(g):
    sig = jax.nn.sigmoid(g)
    return g * sig, sig * (1.0 + g * (1.0 - sig))


def in_vmem(x):
    return pltpu.with_memory_space_constraint(x, pltpu.VMEM)


def in_hbm(x):
    return pltpu.with_memory_space_constraint(x, pltpu.HBM)


WHOLE = pl.BlockSpec(memory_space=pltpu.VMEM)


def front(x, g, w_first, seq, tj):
    lb, block, width = x.shape
    jp = block // seq

    def body(x_ref, g_ref, w_ref, hid_ref, first_ref, wide, turn):
        @pl.when(pl.program_id(0) == 0)
        def _():
            for i in range(lb):
                wide[:, i * width : (i + 1) * width] = x_ref[i]

        res = jnp.dot(w_ref[...], wide[...], preferred_element_type=F32)
        for i in range(lb):
            part = res[:, i * width : (i + 1) * width]
            first_ref[i] = part
            act, _ = gates(g_ref[i].astype(F32))
            turn[pl.ds(i, tj, stride=lb), :] = part * act
        hid_ref[...] = turn[...].reshape(tj // jp, jp, lb, width).astype(BF)

    return pl.pallas_call(
        body,
        grid=(block // tj,),
        in_specs=[
            pl.BlockSpec((lb, block, width), lambda j: (0, 0, 0)),
            pl.BlockSpec((lb, tj, width), lambda j: (0, j, 0)),
            pl.BlockSpec((tj, block), lambda j: (j, 0)),
        ],
        out_specs=[
            pl.BlockSpec((tj // jp, jp, lb, width), lambda j: (j, 1, 0, 0)),
            pl.BlockSpec((lb, tj, width), lambda j: (0, j, 0)),
        ],
        out_shape=[
            pltpu.HBM((seq, 2 * jp, lb, width), BF),
            pltpu.HBM((lb, block, width), F32),
        ],
        scratch_shapes=[
            pltpu.VMEM((block, lb * width), BF),
            pltpu.VMEM((tj * lb, width), F32),
        ],
        name="front",
        compiler_params=pltpu.CompilerParams(vmem_limit_bytes=28 * MIB),
    )(in_hbm(x), in_hbm(g), in_hbm(w_first))


def columns(ref, j, rows):
    return ref[:, j].astype(F32).reshape(rows, LANES).astype(BF)


def pair(ref, j, rows):
    return jnp.concatenate([columns(ref, j, rows), columns(ref, j + 1, rows)], axis=1)


def middle(x_t, w, tj, first_row, into=None):
    seq, lb, width = x_t.shape[0], x_t.shape[2], x_t.shape[3]
    nb = seq * lb
    jp = x_t.shape[1] - first_row
    kept = into is not None

    def body(x_ref, w_ref, *refs):
        out_ref = refs[-1]
        base = pl.program_id(0) * tj if kept else 0
        for j in range(0, tj, 2):
            res = jnp.dot(w_ref[...], pair(x_ref, base + j, nb), preferred_element_type=F32)
            for k in range(2):
                part = res[:, k * width : (k + 1) * width]
                out_ref[:, j + k] = part.reshape(seq, lb, width).astype(BF)

    def block(row):
        return pl.BlockSpec((seq, tj, lb, width), lambda j: (0, row // tj + j, 0, 0))

    return pl.pallas_call(
        body,
        grid=(jp // tj,),
        in_specs=[WHOLE if kept else block(first_row), pl.BlockSpec((nb, nb), lambda j: (0, 0))]
        + [pl.BlockSpec(memory_space=pl.ANY)] * kept,
        out_specs=block(0),
        out_shape=pltpu.HBM(into.shape if kept else (seq, jp, lb, width), BF),
        input_output_aliases={2: 0} if kept else {},
        name="middle_back" if kept else "middle_forward",
        compiler_params=pltpu.CompilerParams(vmem_limit_bytes=16 * MIB),
    )(*([in_vmem(x_t), w, in_hbm(into)] if kept else [in_hbm(x_t), w]))


def second(cot_t, hid_t, first_row, tj):
    seq, jp, lb, width = cot_t.shape
    nb = seq * lb
    steps = jp // tj
    tiles = (nb // 8, nb // LANES, 8, LANES)

    def body(cot_ref, hid_ref, out_ref, acc):
        step = pl.program_id(0)
        total = jnp.zeros((nb, nb), F32)
        for j in range(0, tj, 2):
            total += lax.dot_general(
                pair(cot_ref, step * tj + j, nb), pair(hid_ref, j, nb),
                (((1,), (1,)), ((), ())), preferred_element_type=F32,
            )

        @pl.when(step == 0)
        def _():
            acc[...] = total

        @pl.when(step > 0)
        def _():
            acc[...] += total

        @pl.when(step == steps - 1)
        def _():
            for k in range(nb // LANES):
                part = acc[:, k * LANES : (k + 1) * LANES]
                out_ref[:, k] = part.reshape(nb // 8, 8, LANES).astype(BF)

    return pl.pallas_call(
        body,
        grid=(steps,),
        in_specs=[
            WHOLE,
            pl.BlockSpec((seq, tj, lb, width), lambda j: (0, first_row // tj + j, 0, 0)),
        ],
        out_specs=WHOLE,
        out_shape=pltpu.VMEM(tiles, BF),
        scratch_shapes=[pltpu.VMEM((nb, nb), F32)],
        name="second",
        compiler_params=pltpu.CompilerParams(vmem_limit_bytes=16 * MIB),
    )(in_vmem(cot_t), in_hbm(hid_t))


def pack(x, tj):
    lb, block, width = x.shape

    def body(x_ref, out_ref, turn):
        for i in range(lb):
            turn[pl.ds(i, tj, stride=lb), :] = x_ref[i].astype(F32)
        out_ref[...] = turn[...].reshape(tj, lb, width).astype(BF)

    return pl.pallas_call(
        body,
        grid=(block // tj,),
        in_specs=[pl.BlockSpec((lb, tj, width), lambda j: (0, j, 0))],
        out_specs=pl.BlockSpec((tj, lb, width), lambda j: (j, 0, 0)),
        out_shape=pltpu.HBM((block, lb, width), BF),
        scratch_shapes=[pltpu.VMEM((tj * lb, width), F32)],
        name="pack",
        compiler_params=pltpu.CompilerParams(vmem_limit_bytes=8 * MIB),
    )(in_hbm(x))


def unfold(x, tj):
    block, lb, width = x.shape

    def body(x_ref, out_ref, turn):
        turn[...] = x_ref[...].astype(F32).reshape(tj * lb, width)
        for i in range(lb):
            out_ref[i] = turn[pl.ds(i, tj, stride=lb), :].astype(BF)

    return pl.pallas_call(
        body,
        grid=(block // tj,),
        in_specs=[pl.BlockSpec((tj, lb, width), lambda j: (j, 0, 0))],
        out_specs=pl.BlockSpec((lb, tj, width), lambda j: (0, j, 0)),
        out_shape=pltpu.HBM((lb, block, width), BF),
        scratch_shapes=[pltpu.VMEM((tj * lb, width), F32)],
        name="unfold",
        compiler_params=pltpu.CompilerParams(vmem_limit_bytes=8 * MIB),
    )(x)


def back(where, gh, first, x, g, tj):
    lb, block, width = x.shape
    steps = block // tj
    half = steps // 2
    tiles = block // LANES
    jp = block // gh.shape[0]

    def body(where_ref, gh_ref, first_ref, x_ref, g_ref, gate_ref, gfa_ref, give_ref, own_ref,
             wide, turn):
        step = pl.program_id(0)

        @pl.when(step == 0)
        def _():
            for i in range(lb):
                wide[:, i * width : (i + 1) * width] = x_ref[i]

        turn[...] = gh_ref[...].astype(F32).reshape(tj * lb, width)
        for i in range(lb):
            gh_i = turn[pl.ds(i, tj, stride=lb), :]
            act, slope = gates(g_ref[i].astype(F32))
            gfa_ref[:, i * width : (i + 1) * width] = (gh_i * act).astype(BF)
            gate_ref[i] = (gh_i * first_ref[i] * slope).astype(BF)
        term = lax.dot_general(
            gfa_ref[...], wide[...], (((1,), (1,)), ((), ())), preferred_element_type=F32
        )

        def store(ref):
            for k in range(tiles):
                part = term[:, k * LANES : (k + 1) * LANES]
                ref[:, k] = part.reshape(tj // 8, 8, LANES).astype(BF)

        @pl.when(step < half)
        def _():
            store(give_ref)

        @pl.when(step >= half)
        def _():
            store(own_ref)

    def at(j, where_ref):
        return (j + (1 - where_ref[0]) * half) % steps

    piece = (tj // 8, tiles, 8, LANES)
    grid_spec = pltpu.PrefetchScalarGridSpec(
        num_scalar_prefetch=1,
        grid=(steps,),
        in_specs=[
            pl.BlockSpec((tj // jp, jp, lb, width), lambda j, c: (at(j, c), 0, 0, 0)),
            pl.BlockSpec((lb, tj, width), lambda j, c: (0, at(j, c), 0)),
            pl.BlockSpec((lb, block, width), lambda j, c: (0, 0, 0)),
            pl.BlockSpec((lb, tj, width), lambda j, c: (0, at(j, c), 0)),
        ],
        out_specs=[
            pl.BlockSpec((lb, tj, width), lambda j, c: (0, at(j, c), 0)),
            pl.BlockSpec((tj, lb * width), lambda j, c: (at(j, c), 0)),
            pl.BlockSpec(piece, lambda j, c: (jnp.minimum(j, half - 1), 0, 0, 0)),
            pl.BlockSpec(piece, lambda j, c: (jnp.maximum(j - half, 0), 0, 0, 0)),
        ],
        scratch_shapes=[
            pltpu.VMEM((block, lb * width), BF),
            pltpu.VMEM((tj * lb, width), F32),
        ],
    )
    half_shape = (block // 16, tiles, 8, LANES)
    return pl.pallas_call(
        body,
        grid_spec=grid_spec,
        out_shape=[
            pltpu.HBM((lb, block, width), BF),
            pltpu.HBM((block, lb * width), BF),
            pltpu.HBM(half_shape, BF),
            pltpu.HBM(half_shape, BF),
        ],
        name="back",
        compiler_params=pltpu.CompilerParams(vmem_limit_bytes=28 * MIB),
    )(where, in_hbm(gh), in_hbm(first), in_hbm(x), in_hbm(g))


def back_tokens(gfa, w_first, width):
    block, wide = gfa.shape
    lb = wide // width

    def body(gfa_ref, w_ref, out_ref):
        res = lax.dot_general(
            w_ref[...], gfa_ref[...], (((0,), (0,)), ((), ())), preferred_element_type=F32
        )
        out_ref[0] = res[:, :width].astype(BF)
        out_ref[1] = res[:, width:].astype(BF)

    return pl.pallas_call(
        body,
        grid=(lb // 2,),
        in_specs=[
            pl.BlockSpec((block, 2 * width), lambda i: (0, i)),
            pl.BlockSpec((block, block), lambda i: (0, 0)),
        ],
        out_specs=pl.BlockSpec((2, block, width), lambda i: (i, 0, 0)),
        out_shape=pltpu.HBM((lb, block, width), BF),
        name="back_tokens",
        compiler_params=pltpu.CompilerParams(vmem_limit_bytes=20 * MIB),
    )(in_hbm(gfa), in_hbm(w_first))


def pair_sum(own, taken, second_term):
    chips, tiles = own.shape[:2]

    def body(own_ref, taken_ref, second_ref, out_ref):
        out_ref[:, :tiles] = (own_ref[...].astype(F32) + taken_ref[...].astype(F32)).astype(BF)
        out_ref[:, tiles] = second_ref[...]

    return pl.pallas_call(
        body,
        in_specs=[WHOLE] * 3,
        out_specs=WHOLE,
        out_shape=pltpu.VMEM((chips, tiles + 1, 8, LANES), BF),
        name="pair_sum",
        compiler_params=pltpu.CompilerParams(vmem_limit_bytes=16 * MIB),
    )(own, in_vmem(taken), in_vmem(second_term))


def chip_sum(parts):
    def body(in_ref, out_ref):
        total = jnp.sum(in_ref[...].astype(F32), axis=0).astype(BF)
        out_ref[...] = jnp.broadcast_to(total[None], out_ref.shape)

    return pl.pallas_call(
        body,
        in_specs=[WHOLE],
        out_specs=WHOLE,
        out_shape=pltpu.VMEM(parts.shape, BF),
        name="chip_sum",
        compiler_params=pltpu.CompilerParams(vmem_limit_bytes=12 * MIB),
    )(in_vmem(parts))


def unpack(where, mine, other, block, nb, scale_first, scale_second):
    chips, tiles = mine.shape[0], mine.shape[1] - 1
    lane_tiles = nb // LANES
    half = chips * 8

    def body(where_ref, mine_ref, other_ref, first_ref, second_ref):
        core = where_ref[0]
        for ref, c in ((mine_ref, core), (other_ref, 1 - core)):
            rows = pl.ds(pl.multiple_of(c * half, half), half)
            for k in range(tiles):
                part = ref[:, k].astype(F32) * scale_first
                first_ref[rows, k * LANES : (k + 1) * LANES] = part.reshape(half, LANES)
        both = mine_ref[:, tiles].astype(F32) + other_ref[:, tiles].astype(F32)
        both = (both * scale_second).reshape(chips // lane_tiles, lane_tiles, 8, LANES)
        for k in range(lane_tiles):
            second_ref[:, k * LANES : (k + 1) * LANES] = both[:, k].reshape(-1, LANES)

    return pl.pallas_call(
        body,
        in_specs=[pl.BlockSpec(memory_space=pltpu.SMEM), WHOLE, WHOLE],
        out_specs=[WHOLE, WHOLE],
        out_shape=[
            jax.ShapeDtypeStruct((block, block), F32),
            jax.ShapeDtypeStruct((nb, nb), F32),
        ],
        name="unpack",
        compiler_params=pltpu.CompilerParams(vmem_limit_bytes=16 * MIB),
    )(where, in_vmem(mine), in_vmem(other))


def local(tokens, gate, cotangent, w_first, w_second):
    seq_count = lax.axis_size("seq")
    chan_count = lax.axis_size("ch")
    width = tokens.shape[1]
    block = w_first.shape[0]
    lb = tokens.shape[0] // block
    nb = lb * seq_count
    jp = block // seq_count
    rows = lb * block
    chips = seq_count * chan_count // 2
    same_core = [[2 * k + core for k in range(chips)] for core in range(2)]
    pairs = [(i, i ^ 1) for i in range(chan_count)]
    where = (lax.axis_index("ch") % 2).astype(jnp.int32).reshape(1)

    def exchange(x):
        return lax.all_to_all(x, "seq", split_axis=0, concat_axis=0, tiled=True)

    def chip_exchange(x):
        return lax.all_to_all(
            x, ("seq", "ch"), 0, 0, tiled=True, axis_index_groups=same_core
        )

    x = tokens.reshape(lb, block, width)
    g = gate.reshape(lb, block, width)
    cot = pack(cotangent.reshape(lb, block, width), 256)
    cot_t = exchange(cot.reshape(seq_count, jp, lb, width))
    both, first = front(x, g, w_first, seq_count, 256)
    both = middle(cot_t, w_second.T, 8, 0, both)
    both = exchange(both)
    mixed_t = middle(both, w_second, 8, jp)
    mixed_r = exchange(mixed_t).reshape(block, lb, width)
    grad_gate, gfa, give, own = back(where, both, first, x, g, 256)
    taken = lax.ppermute(give, "ch", pairs)
    second_term = second(cot_t, both, jp, 8)
    part = pair_sum(own, taken, second_term.reshape(chips, 8, LANES))
    grad_tokens = back_tokens(gfa, w_first, width)
    part, grad_tokens, mixed_r = lax.optimization_barrier((part, grad_tokens, mixed_r))
    part = chip_exchange(part)
    mixed = unfold(mixed_r, 256).reshape(rows, width)
    mine = chip_exchange(chip_sum(part))
    other = lax.ppermute(mine, "ch", pairs)
    total_width = width * chan_count
    grad_first, grad_second = unpack(
        where, mine, other, block, nb,
        (nb * total_width) ** -0.5, (block * total_width) ** -0.5,
    )
    return mixed, grad_tokens.reshape(rows, width), grad_gate.reshape(rows, width), grad_first, grad_second


def solution(mesh):
    return jax.shard_map(
        local,
        mesh=mesh,
        in_specs=(P("seq", "ch"), P("seq", "ch"), P("seq", "ch"), P(), P()),
        out_specs=(P("seq", "ch"), P("seq", "ch"), P("seq", "ch"), P(), P()),
        check_vma=False,
    )
```

time: 232 us -> 197 us (0.85)
  blocking collectives: 0 us -> 102 us
  waiting for transfers between devices: 95.3 us -> 25.1 us
  starting transfers between devices: 66.6 us -> 21.8 us
  Pallas kernels: 57.3 us -> 46.7 us
  local copies, waits for them, and re-layouts: 9.16 us -> 0.11 us
    all_to_all x0 -> x3, blocking collectives: none -> 102 us  [the longest x1 56.3 us: exchange(): return lax.all_to_all(x, 'seq', split_axis=0, concat_axis=0, tiled=True)]
    ppermute x17 -> x2, waiting for transfers between devices: 42.8 us -> 0.01 us  [the longest x1 0.01 us: local(): other = lax.ppermute(mine, 'ch', pairs)]
    ppermute x17 -> x2, starting transfers between devices: 31.9 us -> 5.77 us  [the longest x1 3.35 us: local(): other = lax.ppermute(mine, 'ch', pairs)]
    all_to_all x4 -> x2, waiting for transfers between devices: 47.4 us -> 25.1 us  [exchange(): return lax.all_to_all(x, 'seq', split_axis=0, concat_axis=0, tiled=True)]
    all_to_all x4 -> x2, starting transfers between devices: 27.8 us -> 16.1 us  [exchange(): return lax.all_to_all(x, 'seq', split_axis=0, concat_axis=0, tiled=True)]
    pallas_call x8 -> x7, Pallas kernels: 34.4 us -> 23.7 us  [the longest x1 10.3 us: back(): pl.pallas_call(body, grid_spec=grid_spec, out_shape=[pltpu.HBM((lb, block...]
    unnamed x35 -> x5, local copies, waits for them, and re-layouts: 9.16 us -> 0.11 us
    all_to_all x1 -> x0, starting transfers between devices: 6.86 us -> none  [local(): lax.all_to_all(part, ('seq', 'ch'), 0, 0, tiled=True, axis_index_groups=p...]
  transfers between devices with their start and end apart: 22 -> 4, of which waited for: 12 -> 2; matrix products, arithmetic and copies ran while one was open for 1% -> 0% of each run, Pallas kernels for 17% -> 17%
where the time goes in v3:
time: 197 us
  blocking collectives  102 us (52%)
  Pallas kernels  46.7 us (24%)
  waiting for transfers between devices  25.1 us (13%)
  starting transfers between devices  21.8 us (11%)
    all_to_all x1, blocking collectives, exchange(): return lax.all_to_all(x, 'seq', split_axis=0, concat_axis=0, tiled=True)  56.3 us
    all_to_all x2, blocking collectives, chip_exchange(): lax.all_to_all(x, ('seq', 'ch'), 0, 0, tiled=True, axis_index_groups=same...  45.8 us
    all_to_all x2, waiting for transfers between devices, exchange(): return lax.all_to_all(x, 'seq', split_axis=0, concat_axis=0, tiled=True)  25.1 us
    all_to_all x2, starting transfers between devices, exchange(): return lax.all_to_all(x, 'seq', split_axis=0, concat_axis=0, tiled=True)  16.1 us
    pallas_call x1, Pallas kernels, back(): pl.pallas_call(body, grid_spec=grid_spec, out_shape=[pltpu.HBM((lb, block...  10.3 us
    pallas_call x1, Pallas kernels, front(): pl.pallas_call(body, grid=(block // tj,), in_specs=[pl.BlockSpec((lb, blo...  8.21 us
    pallas_call x2, Pallas kernels, middle(): pl.pallas_call(body, grid=(jp // tj,), in_specs=[WHOLE if kept else block...  6.84 us
    pallas_call x1, Pallas kernels, back_tokens(): pl.pallas_call(body, grid=(lb // 2,), in_specs=[pl.BlockSpec((block, 2 *...  6.25 us
  transfers between devices with their start and end apart: 4, of which 2 were waited for; matrix products, arithmetic and copies ran while one was open for 0% of the time, Pallas kernels for 17%

profile of v3, /device:TPU:1, one launch (start us, length us, event | category | flops | bytes accessed | tf_op | source)
XLA Modules:
  0.0 196.5 jit_solution(3519186588050038217)
XLA Ops:
  0.6 4.4 %pack.1 = bf16[1024,8,128]{2,1,0:T(8,128)(2,1)} custom-call(bf16[8,1024,128]{2,1,0:T(8,128)(2,1)} %bitcast.19), custom_call_target="tpu_custom_call" | custom-call | tf_op jit(solution)/shard_map/pack/pallas_call | solution.py:164
  5.0 0.0 copy-start.1
  5.0 11.3 %all-to-all-start = ((bf16[32,32,8,128]{3,2,1,0:T(8,128)(2,1)}), bf16[32,32,8,128]{3,2,1,0:T(8,128)(2,1)S(1)}, u32[]{:S(2)}, u32[]{:S(2)}) async-start(bf16[32,32,8,128]{3,2,1,0:T(8,128)(2,1)} %bitcast.17), calls=%async_computation | async-start | bytes 4194304 | tf_op jit(solution)/shard_map/all_to_all | solution.py:376
  16.3 0.0 copy-done.1
  16.3 0.1 copy.11
  16.4 8.2 %front.1 = (bf16[32,64,8,128]{3,2,1,0:T(8,128)(2,1)}, f32[8,1024,128]{2,1,0:T(8,128)}) custom-call(bf16[8,1024,128]{2,1,0:T(8,128)(2,1)} %bitcast.13, bf16[8,1024,128]{2,1,0:T(8,128)(2,1)} %bitcast.15, bf16[1024,1024]{1,0:T(8,128)(2,1)} %w_ref.4), custom_call_target="tpu_custom_call" | custom-call | tf_op jit(solution)/shard_map/front/pallas_call | solution.py:48
  24.6 20.1 %all-to-all-done.x_ref.cot_ref = bf16[32,32,8,128]{3,2,1,0:T(8,128)(2,1)S(1)} async-done(((bf16[32,32,8,128]{3,2,1,0:T(8,128)(2,1)}), bf16[32,32,8,128]{3,2,1,0:T(8,128)(2,1)S(1)}, u32[]{:S(2)}, u32[]{:S(2)}) %all-to-all-start) | async-done | bytes 2097184 | tf_op jit(solution)/shard_map/all_to_all | solution.py:376
  44.7 2.5 %middle_back.1 = bf16[32,64,8,128]{3,2,1,0:T(8,128)(2,1)} custom-call(bf16[32,32,8,128]{3,2,1,0:T(8,128)(2,1)S(1)} %all-to-all-done.x_ref.cot_ref, bf16[256,256]{1,0:T(8,128)(2,1)S(1)} %bitcast.12, bf16[32,64,8,128]{3,2,1,0:T(8,128)(2,1)} %get-tuple-element.16.refs_0_), custom_call_target="tpu_custom_call", output_to_operand_aliasing={{}: (2, {})} | custom-call | tf_op jit(solution)/shard_map/middle_back/pallas_call | solution.py:99
  47.3 56.3 %all_to_all.25.gh_ref.hid_ref.x_ref = bf16[32,64,8,128]{3,2,1,0:T(8,128)(2,1)} all-to-all(bf16[32,64,8,128]{3,2,1,0:T(8,128)(2,1)} %middle_back.1), channel_id=1, replica_groups=mesh['seq'=32,'ch'=4] {'seq'}, dimensions={0} | all-to-all | bytes 8388608 | tf_op jit(solution)/shard_map/all_to_all | solution.py:376
  103.6 4.3 %middle_forward.1 = bf16[32,32,8,128]{3,2,1,0:T(8,128)(2,1)} custom-call(bf16[32,64,8,128]{3,2,1,0:T(8,128)(2,1)} %all_to_all.25.gh_ref.hid_ref.x_ref, bf16[256,256]{1,0:T(8,128)(2,1)S(1)} %copy-done.1), custom_call_target="tpu_custom_call" | custom-call | tf_op jit(solution)/shard_map/middle_forward/pallas_call | solution.py:99
  107.9 4.8 %all-to-all-start.2 = ((bf16[32,32,8,128]{3,2,1,0:T(8,128)(2,1)}), bf16[32,32,8,128]{3,2,1,0:T(8,128)(2,1)}, u32[]{:S(2)}, u32[]{:S(2)}) async-start(bf16[32,32,8,128]{3,2,1,0:T(8,128)(2,1)} %middle_forward.1), calls=%async_computation.2 | async-start | bytes 4194304 | tf_op jit(solution)/shard_map/all_to_all | solution.py:376
  112.7 10.3 %back.1 = (bf16[8,1024,128]{2,1,0:T(8,128)(2,1)}, bf16[1024,1024]{1,0:T(8,128)(2,1)}, bf16[64,8,8,128]{3,2,1,0:T(8,128)(2,1)}, bf16[64,8,8,128]{3,2,1,0:T(8,128)(2,1)}) custom-call(s32[1]{0:T(128)} %bitcast.where_ref, bf16[32,64,8,128]{3,2,1,0:T(8,128)(2,1)} %all_to_all.25.gh_ref.hid_ref.x_ref, f32[8,1024,128]{2,1,0:T(8,128)} %get-tuple-element.17.first_ref, ...), custom_call_target="tpu_custom_call" | custom-call | tf_op jit(solution)/shard_map/back/pallas_call | solution.py:260
  123.0 2.4 %collective-permute-start = (bf16[64,8,8,128]{3,2,1,0:T(8,128)(2,1)}, bf16[64,8,8,128]{3,2,1,0:T(8,128)(2,1)S(1)}, u32[]{:S(2)}, u32[]{:S(2)}) collective-permute-start(bf16[64,8,8,128]{3,2,1,0:T(8,128)(2,1)} %get-tuple-element.19), channel_id=1, source_target_pairs={{0,1},{1,0},{2,3},{3,2},{4,5},{5,4},{6,7},{7,6},{8,9},{9,8},{10,11... | collective-permute-start | bytes 3145736 | tf_op jit(solution)/shard_map/ppermute | solution.py:393
  125.4 6.2 %back_tokens.1 = bf16[8,1024,128]{2,1,0:T(8,128)(2,1)} custom-call(bf16[1024,1024]{1,0:T(8,128)(2,1)} %get-tuple-element.20.gfa_ref, bf16[1024,1024]{1,0:T(8,128)(2,1)} %w_ref.4), custom_call_target="tpu_custom_call" | custom-call | tf_op jit(solution)/shard_map/back_tokens/pallas_call | solution.py:285
  131.7 0.0 copy-start
  131.7 3.4 %second.1 = bf16[32,2,8,128]{3,2,1,0:T(8,128)(2,1)S(1)} custom-call(bf16[32,32,8,128]{3,2,1,0:T(8,128)(2,1)S(1)} %all-to-all-done.x_ref.cot_ref, bf16[32,64,8,128]{3,2,1,0:T(8,128)(2,1)} %all_to_all.25.gh_ref.hid_ref.x_ref), custom_call_target="tpu_custom_call" | custom-call | tf_op jit(solution)/shard_map/second/pallas_call | solution.py:141
  135.0 0.0 collective-permute-done.taken_ref
  135.0 0.0 copy-done
  135.1 0.3 pair_sum.1
  135.3 5.0 %all-to-all-done.2 = bf16[32,32,8,128]{3,2,1,0:T(8,128)(2,1)} async-done(((bf16[32,32,8,128]{3,2,1,0:T(8,128)(2,1)}), bf16[32,32,8,128]{3,2,1,0:T(8,128)(2,1)}, u32[]{:S(2)}, u32[]{:S(2)}) %all-to-all-start.2) | async-done | bytes 2097184 | tf_op jit(solution)/shard_map/all_to_all | solution.py:376
  140.3 20.4 %all_to_all.26.in_ref = bf16[64,9,8,128]{3,2,1,0:T(8,128)(2,1)S(1)} all-to-all(bf16[64,9,8,128]{3,2,1,0:T(8,128)(2,1)S(1)} %pair_sum.1), channel_id=1, replica_groups={{0,2,4,6,8,10,12,14,16,18,20,22,24,26,28,30,32,34,36,38,40,42,44,46,48,..., dimensions={0} | all-to-all | bytes 2359296 | tf_op jit(solution)/shard_map/all_to_all | solution.py:379
  160.7 0.2 chip_sum.1
  160.9 25.4 %all_to_all.27.mine_ref = bf16[64,9,8,128]{3,2,1,0:T(8,128)(2,1)S(1)} all-to-all(bf16[64,9,8,128]{3,2,1,0:T(8,128)(2,1)S(1)} %chip_sum.1), channel_id=1, replica_groups={{0,2,4,6,8,10,12,14,16,18,20,22,24,26,28,30,32,34,36,38,40,42,44,46,48,..., dimensions={0} | all-to-all | bytes 2359296 | tf_op jit(solution)/shard_map/all_to_all | solution.py:379
  186.3 3.3 %collective-permute-start.1 = (bf16[64,9,8,128]{3,2,1,0:T(8,128)(2,1)S(1)}, bf16[64,9,8,128]{3,2,1,0:T(8,128)(2,1)S(1)}, u32[]{:S(2)}, u32[]{:S(2)}) collective-permute-start(bf16[64,9,8,128]{3,2,1,0:T(8,128)(2,1)S(1)} %all_to_all.27.mine_ref), channel_id=1, source_target_pairs={{0,1},{1,0},{2,3},{3,2},{4,5},{5,4},{6,7},{7,6},{8,9},{9,8},{10,11... | collective-permute-start | bytes 3538952 | tf_op jit(solution)/shard_map/ppermute | solution.py:401
  189.7 4.2 %unfold.1 = bf16[8,1024,128]{2,1,0:T(8,128)(2,1)} custom-call(bf16[1024,8,128]{2,1,0:T(8,128)(2,1)} %bitcast.7.x_ref), custom_call_target="tpu_custom_call" | custom-call | tf_op jit(solution)/shard_map/unfold/pallas_call | solution.py:184
  193.9 0.0 collective-permute-done.1.other_ref
  193.9 2.7 %unpack.1 = (f32[1024,1024]{1,0:T(8,128)}, f32[256,256]{1,0:T(8,128)}) custom-call(s32[1]{0:T(128)} %bitcast.where_ref, bf16[64,9,8,128]{3,2,1,0:T(8,128)(2,1)S(1)} %all_to_all.27.mine_ref, bf16[64,9,8,128]{3,2,1,0:T(8,128)(2,1)S(1)} %collective-permute-done.1.other_ref), custom_call_target="tpu_custom_call" | custom-call | tf_op jit(solution)/shard_map/unpack/pallas_call | solution.py:348
Async XLA Ops:
  5.0 11.3 %copy-start.1 = (bf16[256,256]{1,0:T(8,128)(2,1)S(1)}, bf16[256,256]{1,0:T(8,128)(2,1)}, u32[]{:S(2)}) copy-start(bf16[256,256]{1,0:T(8,128)(2,1)} %w_ref.5) | copy-start | bytes 393220
  5.0 39.7 %all-to-all-start = ((bf16[32,32,8,128]{3,2,1,0:T(8,128)(2,1)}), bf16[32,32,8,128]{3,2,1,0:T(8,128)(2,1)S(1)}, u32[]{:S(2)}, u32[]{:S(2)}) async-start(bf16[32,32,8,128]{3,2,1,0:T(8,128)(2,1)} %bitcast.17), calls=%async_computation | async-start | bytes 4194304 | tf_op jit(solution)/shard_map/all_to_all | solution.py:376
  107.9 32.4 %all-to-all-start.2 = ((bf16[32,32,8,128]{3,2,1,0:T(8,128)(2,1)}), bf16[32,32,8,128]{3,2,1,0:T(8,128)(2,1)}, u32[]{:S(2)}, u32[]{:S(2)}) async-start(bf16[32,32,8,128]{3,2,1,0:T(8,128)(2,1)} %middle_forward.1), calls=%async_computation.2 | async-start | bytes 4194304 | tf_op jit(solution)/shard_map/all_to_all | solution.py:376
  123.0 12.1 %collective-permute-start = (bf16[64,8,8,128]{3,2,1,0:T(8,128)(2,1)}, bf16[64,8,8,128]{3,2,1,0:T(8,128)(2,1)S(1)}, u32[]{:S(2)}, u32[]{:S(2)}) collective-permute-start(bf16[64,8,8,128]{3,2,1,0:T(8,128)(2,1)} %get-tuple-element.19), channel_id=1, source_target_pairs={{0,1},{1,0},{2,3},{3,2},{4,5},{5,4},{6,7},{7,6},{8,9},{9,8},{10,11... | collective-permute-start | bytes 3145736 | tf_op jit(solution)/shard_map/ppermute | solution.py:393
  131.7 3.4 %copy-start = (bf16[64,8,8,128]{3,2,1,0:T(8,128)(2,1)S(1)}, bf16[64,8,8,128]{3,2,1,0:T(8,128)(2,1)}, u32[]{:S(2)}) copy-start(bf16[64,8,8,128]{3,2,1,0:T(8,128)(2,1)} %get-tuple-element.18.own_ref) | copy-start | bytes 3145732
  186.3 7.5 %collective-permute-start.1 = (bf16[64,9,8,128]{3,2,1,0:T(8,128)(2,1)S(1)}, bf16[64,9,8,128]{3,2,1,0:T(8,128)(2,1)S(1)}, u32[]{:S(2)}, u32[]{:S(2)}) collective-permute-start(bf16[64,9,8,128]{3,2,1,0:T(8,128)(2,1)S(1)} %all_to_all.27.mine_ref), channel_id=1, source_target_pairs={{0,1},{1,0},{2,3},{3,2},{4,5},{5,4},{6,7},{7,6},{8,9},{9,8},{10,11... | collective-permute-start | bytes 3538952 | tf_op jit(solution)/shard_map/ppermute | solution.py:401
